TPU v7x, 32 devices: a whole 2x2x4 slice. The times are simulated.
32 devices in a mesh: head: 4 (over y, core), blk: 8 (over z, x).
Axes of the slice: x: 2, y: 2, z: 4, core: 2. Of those that a mesh axis runs over, the one named last changes fastest.
Arguments:
- tokens: bfloat16 [4096, 2048], P(('head', 'blk')), may hold values from -50 to 50
- out_grad: bfloat16 [4096, 2048], P(('head', 'blk')), may hold values from -6 to 6
- seq_lengths: int32 [8], replicated, may hold values from 1 to 2048, 4096 in all
- block_deal: int32 [16], replicated, may hold values from 0 to 15, as said below
- norm_gain: bfloat16 [2048], P('blk'), may hold values from 0.5 to 1.5
- q_weight: bfloat16 [2048, 2048], P('blk', 'head'), may hold values from -0.125 to 0.125
- key_projection_weight: bfloat16 [2048, 1024], P('blk', 'head'), may hold values from -0.125 to 0.125
- value_projection_weight: bfloat16 [2048, 1024], P('blk', 'head'), may hold values from -0.125 to 0.125
- q_gain: bfloat16 [128], P('blk'), may hold values from 0.5 to 1.5
- k_gain: bfloat16 [128], P('blk'), may hold values from 0.5 to 1.5
- o_weight: bfloat16 [2048, 2048], P('head', 'blk'), may hold values from -0.75 to 0.75
- mlp_gain: bfloat16 [2048], P('blk'), may hold values from 0.5 to 1.5
- gate_weight: bfloat16 [2048, 6144], P('blk', 'head'), may hold values from -0.125 to 0.125
- up_weight: bfloat16 [2048, 6144], P('blk', 'head'), may hold values from -0.125 to 0.125
- down_weight: bfloat16 [6144, 2048], P('head', 'blk'), may hold values from -0.078125 to 0.078125
Outputs:
- block_out: bfloat16 [4096, 2048], P(('head', 'blk'))
- in_grad: float32 [4096, 2048], P(('head', 'blk'))
- norm_gain_grad: float32 [2048], P(('head', 'blk'))
- q_weight_grad: float32 [2048, 2048], P('blk', 'head')
- k_weight_grad: float32 [2048, 1024], P('blk', 'head')
- v_weight_grad: float32 [2048, 1024], P('blk', 'head')
- q_gain_grad: float32 [128], P(('head', 'blk'))
- k_gain_grad: float32 [128], P(('head', 'blk'))
- o_weight_grad: float32 [2048, 2048], P('head', 'blk')
- mlp_gain_grad: float32 [2048], P(('head', 'blk'))
- gate_weight_grad: float32 [2048, 6144], P('blk', 'head')
- up_weight_grad: float32 [2048, 6144], P('blk', 'head')
- down_weight_grad: float32 [6144, 2048], P('head', 'blk')
Inputs may be any that keep to these rules, and one draw needn't show every extreme that they name: `seq_lengths`: the lengths sum to 4096; the longest has exactly 2048 tokens. `block_deal`: a permutation of 0 to 15 in which entries 2 b and 2 b + 1 sum to 15.
All inputs are finite; a program needn't handle non-finite values.
Results may differ from a plain program's by a relative error of at most 0.035.
Values may be sent and summed in bfloat16 or wider, within the bound.
No kernel may reach another device: no remote copies, remote signals or barrier semaphores. Data moves between devices by JAX's collectives and lax.ppermute only.
A program may use at most 320 MiB of HBM per device.

v0:
```python
import jax
import jax.numpy as jnp
from jax import lax
from jax.sharding import PartitionSpec as P

HEAD_SIZE = 128


EPSILON = 1e-06
ROPE_BASE = 1000000.0
MASKED_SCORE = -1e30


def shifted(value, axis, steps):
    count = lax.axis_size(axis)
    pairs = [(source, (source + steps) % count) for source in range(count)]
    return lax.ppermute(value, axis, pairs)


def rms_norm(values_in, gain_vec):
    mean_square = jnp.mean(values_in * values_in, axis=-1, keepdims=True)
    return values_in * lax.rsqrt(mean_square + EPSILON) * gain_vec


def rotate(head_rows, places):
    head_width = head_rows.shape[-1]
    half_width = head_width // 2
    frequency = jnp.power(
        ROPE_BASE, -jnp.arange(half_width, dtype=jnp.float32) * (2.0 / head_width)
    )
    angles = places.astype(jnp.float32)[:, None] * frequency[None, :]
    cosine = jnp.cos(angles)[:, None, :]
    sine_part = jnp.sin(angles)[:, None, :]
    first_half = head_rows[..., :half_width]
    second = head_rows[..., half_width:]
    return jnp.concatenate(
        [first_half * cosine - second * sine_part, second * cosine + first_half * sine_part],
        axis=-1,
    )


def head_shape(raw_rows, gain_vec, places, factor):
    row_count = raw_rows.shape[0]
    head_rows = raw_rows.reshape(row_count, -1, gain_vec.shape[0])
    return (rotate(rms_norm(head_rows, gain_vec), places) * factor).reshape(row_count, -1)


def natural_places(blk_ids, group_rows, block_deal, seq_lengths, head_count, tok_dev):
    half_heads = head_count // 2
    source = group_rows // tok_dev
    within = group_rows % tok_dev
    entry_index = 2 * blk_ids + source // half_heads
    span_table = jnp.arange(block_deal.shape[0], dtype=jnp.int32)
    span_ids = jnp.sum(
        jnp.where(entry_index[:, None] == span_table[None, :], block_deal[None, :], 0),
        axis=1,
        dtype=jnp.int32,
    )
    natural = span_ids * (half_heads * tok_dev) + source % half_heads * tok_dev + within
    seq_ends = jnp.cumsum(seq_lengths, dtype=jnp.int32)
    seq_start = jnp.max(
        jnp.where(seq_ends[None, :] <= natural[:, None], seq_ends[None, :], 0), axis=1
    )
    return (natural, seq_start)


def swiglu(gate_in, up_in):
    return jax.nn.silu(gate_in) * up_in


def contract_rows(left_side, right_side):
    return lax.dot_general(
        left_side, right_side, (((0,), (0,)), ((), ())), preferred_element_type=jnp.float32
    )


def contract_cols(left_side, right_side):
    return lax.dot_general(
        left_side, right_side, (((1,), (1,)), ((), ())), preferred_element_type=jnp.float32
    )


def shards(
    tokens,
    out_grad,
    seq_lengths,
    block_deal,
    norm_gain,
    q_weight,
    key_projection_weight,
    value_projection_weight,
    q_gain,
    k_gain,
    o_weight,
    mlp_gain,
    gate_weight,
    up_weight,
    down_weight,
):
    head_count = lax.axis_size("head")
    blk_count = lax.axis_size("blk")
    tok_dev = tokens.shape[0]
    group_size = head_count * tok_dev
    blk_index = lax.axis_index("blk")
    (
        gain_one,
        q_cols,
        k_cols,
        v_cols,
        gain_q,
        gain_k,
        o_rows,
        gain_two,
        gate_cols,
        up_cols,
        down_rows,
    ) = (
        lax.all_gather(norm_gain, "blk", axis=0, tiled=True),
        lax.all_gather(q_weight, "blk", axis=0, tiled=True),
        lax.all_gather(key_projection_weight, "blk", axis=0, tiled=True),
        lax.all_gather(value_projection_weight, "blk", axis=0, tiled=True),
        lax.all_gather(q_gain, "blk", axis=0, tiled=True),
        lax.all_gather(k_gain, "blk", axis=0, tiled=True),
        lax.all_gather(o_weight, "blk", axis=1, tiled=True),
        lax.all_gather(mlp_gain, "blk", axis=0, tiled=True),
        lax.all_gather(gate_weight, "blk", axis=0, tiled=True),
        lax.all_gather(up_weight, "blk", axis=0, tiled=True),
        lax.all_gather(down_weight, "blk", axis=1, tiled=True),
    )
    gain_one = gain_one.astype(jnp.float32)
    gain_two = gain_two.astype(jnp.float32)
    gain_q = gain_q.astype(jnp.float32)
    gain_k = gain_k.astype(jnp.float32)
    kv_heads = k_cols.shape[1] // HEAD_SIZE
    kv_width = kv_heads * HEAD_SIZE
    pair_count = q_cols.shape[1] // kv_width
    factor = HEAD_SIZE ** (-0.5)
    query_nat, query_start = natural_places(
        blk_index + jnp.zeros((group_size,), jnp.int32),
        jnp.arange(group_size, dtype=jnp.int32),
        block_deal,
        seq_lengths,
        head_count,
        tok_dev,
    )
    query_place = query_nat - query_start

    def key_places(first_row, row_count):
        key_index = first_row + jnp.arange(row_count, dtype=jnp.int32)
        natural, unused = natural_places(
            key_index // group_size,
            key_index % group_size,
            block_deal,
            seq_lengths,
            head_count,
            tok_dev,
        )
        return natural

    local_rows = tokens.astype(jnp.float32)
    input_rows = lax.all_gather(tokens, "head", axis=0, tiled=True).astype(jnp.float32)
    normed = rms_norm(input_rows, gain_one).astype(jnp.bfloat16)
    q_raw = jnp.dot(normed, q_cols, preferred_element_type=jnp.float32)
    k_raw = jnp.dot(normed, k_cols, preferred_element_type=jnp.float32)
    v_raw = jnp.dot(normed, v_cols, preferred_element_type=jnp.float32)
    query_matrix = head_shape(q_raw, gain_q, query_place, factor).astype(jnp.bfloat16)
    rows_of_keys = head_shape(k_raw, gain_k, query_place, 1.0).astype(jnp.bfloat16)
    query_layout = query_matrix.reshape(group_size, kv_heads, pair_count, HEAD_SIZE)
    kv_pair = jnp.stack([rows_of_keys, v_raw.astype(jnp.bfloat16)])

    def tile_setup(key_count, key_piece, key_nat):
        allowed = (key_nat[None, :] <= query_nat[:, None]) & (
            key_nat[None, :] >= query_start[:, None]
        )
        key_layout = key_piece[0].reshape(key_count, kv_heads, HEAD_SIZE)
        value_layout = key_piece[1].reshape(key_count, kv_heads, HEAD_SIZE)
        scores = jnp.einsum(
            "qjgd,kjd->qjgk", query_layout, key_layout, preferred_element_type=jnp.float32
        )
        return (allowed[:, None, None, :], query_layout, key_layout, value_layout, scores)

    def run_tiles(tile_work, running, key_piece, key_nat, base_row):
        key_count = key_piece.shape[1]
        return tile_work(running, 0, group_size, 0, key_count, key_piece, key_nat, base_row)

    def attend_tile(
        running, query_first, query_count, key_first, key_count, key_piece, key_nat, base_row
    ):
        peak_scores, totals, accumulated = running
        allowed, part_query, key_layout, value_layout, scores = tile_setup(
            key_count, key_piece, key_nat
        )
        new_peak = jnp.maximum(
            peak_scores, jnp.max(jnp.where(allowed, scores, MASKED_SCORE), axis=-1)
        )
        weights = jnp.where(allowed, jnp.exp(scores - new_peak[..., None]), 0.0)
        new_total = jnp.sum(weights, axis=-1)
        new_accum = jnp.einsum(
            "qjgk,kjd->qjgd",
            weights.astype(jnp.bfloat16),
            value_layout,
            preferred_element_type=jnp.float32,
        )
        return (new_peak, new_total, new_accum)

    start_state = (
        jnp.full((group_size, kv_heads, pair_count), MASKED_SCORE, jnp.float32),
        jnp.zeros((group_size, kv_heads, pair_count), jnp.float32),
        jnp.zeros((group_size, kv_heads, pair_count, HEAD_SIZE), jnp.float32),
    )
    key_piece = lax.all_gather(kv_pair, "blk", axis=1, tiled=True)
    peak_scores, totals, accumulated = run_tiles(
        attend_tile, start_state, key_piece, key_places(jnp.int32(0), key_piece.shape[1]), 0
    )
    attended = accumulated / totals[..., None]
    log_total = peak_scores + jnp.log(totals)
    attn_low = attended.reshape(group_size, -1).astype(jnp.bfloat16)
    residual = local_rows + lax.psum_scatter(
        jnp.dot(attn_low, o_rows, preferred_element_type=jnp.float32).astype(jnp.bfloat16),
        "head",
        scatter_dimension=0,
        tiled=True,
    ).astype(jnp.float32)
    mlp_rows = lax.all_gather(
        rms_norm(residual, gain_two).astype(jnp.bfloat16), "head", axis=0, tiled=True
    )
    gate_act = jnp.dot(mlp_rows, gate_cols, preferred_element_type=jnp.float32)
    up_act = jnp.dot(mlp_rows, up_cols, preferred_element_type=jnp.float32)
    hidden = swiglu(gate_act, up_act).astype(jnp.bfloat16)
    block_out = (
        residual
        + lax.psum_scatter(
            jnp.dot(hidden, down_rows, preferred_element_type=jnp.float32).astype(jnp.bfloat16),
            "head",
            scatter_dimension=0,
            tiled=True,
        ).astype(jnp.float32)
    ).astype(jnp.bfloat16)
    grad_rows = lax.all_gather(out_grad, "head", axis=0, tiled=True)
    down_wgrad = contract_rows(hidden, grad_rows)
    hidden_grad = contract_cols(grad_rows, down_rows)
    unused, swiglu_pull = jax.vjp(swiglu, gate_act, up_act)
    gate_grad, up_grad = swiglu_pull(hidden_grad)
    gate_low = gate_grad.astype(jnp.bfloat16)
    up_low = up_grad.astype(jnp.bfloat16)
    gate_wgrad = contract_rows(mlp_rows, gate_low)
    up_wgrad = contract_rows(mlp_rows, up_low)
    mlp_in_grad = lax.psum_scatter(
        (contract_cols(gate_low, gate_cols) + contract_cols(up_low, up_cols)).astype(jnp.bfloat16),
        "head",
        scatter_dimension=0,
        tiled=True,
    ).astype(jnp.float32)
    unused, norm_pull = jax.vjp(rms_norm, residual, gain_two)
    resid_norm_grad, gain_two_part = norm_pull(mlp_in_grad)
    residual_grad = out_grad.astype(jnp.float32) + resid_norm_grad
    branch_rows = lax.all_gather(residual_grad.astype(jnp.bfloat16), "head", axis=0, tiled=True)
    o_wgrad = contract_rows(attn_low, branch_rows)
    attn_grad = contract_cols(branch_rows, o_rows).astype(jnp.bfloat16)
    grad_view = attn_grad.reshape(group_size, kv_heads, pair_count, HEAD_SIZE)
    deltas = jnp.sum(grad_view.astype(jnp.float32) * attended, axis=-1)

    def score_back(key_count, key_piece, key_nat):
        allowed, part_query, key_layout, value_layout, scores = tile_setup(
            key_count, key_piece, key_nat
        )
        probabilities = jnp.where(allowed, jnp.exp(scores - log_total[..., None]), 0.0)
        prob_grad = jnp.einsum(
            "qjgd,kjd->qjgk", grad_view, value_layout, preferred_element_type=jnp.float32
        )
        score_grad = (probabilities * (prob_grad - deltas[..., None])).astype(jnp.bfloat16)
        return (part_query, grad_view, key_layout, probabilities, score_grad)

    def reverse_tile(
        running, query_first, query_count, key_first, key_count, key_piece, key_nat, base_row
    ):
        query_grad, key_grads = running
        part_query, part_grad, key_layout, probabilities, score_grad = score_back(
            key_count, key_piece, key_nat
        )
        new_query = query_grad + jnp.einsum(
            "qjgk,kjd->qjgd", score_grad, key_layout, preferred_element_type=jnp.float32
        )
        key_part = jnp.einsum(
            "qjgk,qjgd->kjd", score_grad, part_query, preferred_element_type=jnp.float32
        ).reshape(key_count, -1)
        value_part = jnp.einsum(
            "qjgk,qjgd->kjd",
            probabilities.astype(jnp.bfloat16),
            part_grad,
            preferred_element_type=jnp.float32,
        ).reshape(key_count, -1)
        old_grads = key_grads
        key_grads = old_grads + jnp.stack([key_part, value_part])
        return (new_query, key_grads)

    grad_start = jnp.zeros((group_size, kv_heads, pair_count, HEAD_SIZE), jnp.float32)

    def back_step(cycle_step, carried):
        query_grad, kv_now, grads_now = carried
        source_blk = (blk_index - cycle_step) % blk_count
        key_nat = key_places(source_blk * group_size, group_size)
        query_grad, grads_now = run_tiles(reverse_tile, (query_grad, grads_now), kv_now, key_nat, 0)
        kv_next = shifted(kv_now, "blk", 1)
        grads_next = shifted(grads_now.astype(jnp.bfloat16), "blk", 1).astype(grads_now.dtype)
        return (query_grad, kv_next, grads_next)

    query_grad, unused_kv, key_grads = lax.fori_loop(
        0,
        blk_count,
        back_step,
        (grad_start, kv_pair, jnp.zeros((2, group_size, kv_width), jnp.float32)),
    )
    query_round = lax.optimization_barrier(
        query_grad.reshape(group_size, -1).astype(jnp.bfloat16)
    ).astype(jnp.float32)
    unused, query_pull = jax.vjp(
        lambda raw_rows, gain_vec: head_shape(raw_rows, gain_vec, query_place, factor),
        q_raw,
        gain_q,
    )
    q_raw_grad, gain_q_part = query_pull(query_round)
    key_round = lax.optimization_barrier(key_grads[0].astype(jnp.bfloat16)).astype(jnp.float32)
    unused, key_pull = jax.vjp(
        lambda raw_rows, gain_vec: head_shape(raw_rows, gain_vec, query_place, 1.0), k_raw, gain_k
    )
    k_raw_grad, gain_k_part = key_pull(key_round)
    q_low = q_raw_grad.astype(jnp.bfloat16)
    k_low = k_raw_grad.astype(jnp.bfloat16)
    v_low = key_grads[1].astype(jnp.bfloat16)
    q_wgrad = contract_rows(normed, q_low)
    k_wgrad = contract_rows(normed, k_low)
    v_wgrad = contract_rows(normed, v_low)
    input_terms = (
        contract_cols(q_low, q_cols) + contract_cols(k_low, k_cols) + contract_cols(v_low, v_cols)
    )
    unused, gain_pull = jax.vjp(lambda gain_vec: rms_norm(input_rows, gain_vec), gain_one)
    (gain_one_part,) = gain_pull(input_terms)
    input_grad, gain_one_head, gain_two_head, gain_q_head, gain_k_head = (
        lax.psum_scatter(
            input_terms.astype(jnp.bfloat16), "head", scatter_dimension=0, tiled=True
        ).astype(jnp.float32),
        lax.psum_scatter(
            gain_one_part.astype(jnp.bfloat16), "head", scatter_dimension=0, tiled=True
        ).astype(jnp.float32),
        lax.psum_scatter(
            gain_two_part.astype(jnp.bfloat16), "head", scatter_dimension=0, tiled=True
        ).astype(jnp.float32),
        lax.psum_scatter(
            gain_q_part.astype(jnp.bfloat16), "head", scatter_dimension=0, tiled=True
        ).astype(jnp.float32),
        lax.psum_scatter(
            gain_k_part.astype(jnp.bfloat16), "head", scatter_dimension=0, tiled=True
        ).astype(jnp.float32),
    )
    unused, input_pull = jax.vjp(lambda row_values: rms_norm(row_values, gain_one), local_rows)
    (input_norm_grad,) = input_pull(input_grad)
    in_grad = residual_grad + input_norm_grad
    results = (
        lax.psum_scatter(
            gain_one_head.astype(jnp.bfloat16), "blk", scatter_dimension=0, tiled=True
        ).astype(jnp.float32),
        lax.psum_scatter(
            q_wgrad.astype(jnp.bfloat16), "blk", scatter_dimension=0, tiled=True
        ).astype(jnp.float32),
        lax.psum_scatter(
            k_wgrad.astype(jnp.bfloat16), "blk", scatter_dimension=0, tiled=True
        ).astype(jnp.float32),
        lax.psum_scatter(
            v_wgrad.astype(jnp.bfloat16), "blk", scatter_dimension=0, tiled=True
        ).astype(jnp.float32),
        lax.psum_scatter(
            gain_q_head.astype(jnp.bfloat16), "blk", scatter_dimension=0, tiled=True
        ).astype(jnp.float32),
        lax.psum_scatter(
            gain_k_head.astype(jnp.bfloat16), "blk", scatter_dimension=0, tiled=True
        ).astype(jnp.float32),
        lax.psum_scatter(
            o_wgrad.astype(jnp.bfloat16), "blk", scatter_dimension=1, tiled=True
        ).astype(jnp.float32),
        lax.psum_scatter(
            gain_two_head.astype(jnp.bfloat16), "blk", scatter_dimension=0, tiled=True
        ).astype(jnp.float32),
        lax.psum_scatter(
            gate_wgrad.astype(jnp.bfloat16), "blk", scatter_dimension=0, tiled=True
        ).astype(jnp.float32),
        lax.psum_scatter(
            up_wgrad.astype(jnp.bfloat16), "blk", scatter_dimension=0, tiled=True
        ).astype(jnp.float32),
        lax.psum_scatter(
            down_wgrad.astype(jnp.bfloat16), "blk", scatter_dimension=1, tiled=True
        ).astype(jnp.float32),
    )
    return (
        block_out,
        in_grad,
        results[0],
        results[1],
        results[2],
        results[3],
        results[4],
        results[5],
        results[6],
        results[7],
        results[8],
        results[9],
        results[10],
    )


def solution(mesh):
    return jax.shard_map(
        shards,
        mesh=mesh,
        in_specs=(
            P(("head", "blk"), None),
            P(("head", "blk"), None),
            P(),
            P(),
            P("blk"),
            P("blk", "head"),
            P("blk", "head"),
            P("blk", "head"),
            P("blk"),
            P("blk"),
            P("head", "blk"),
            P("blk"),
            P("blk", "head"),
            P("blk", "head"),
            P("head", "blk"),
        ),
        out_specs=(
            P(("head", "blk"), None),
            P(("head", "blk"), None),
            P(("head", "blk")),
            P("blk", "head"),
            P("blk", "head"),
            P("blk", "head"),
            P(("head", "blk")),
            P(("head", "blk")),
            P("head", "blk"),
            P(("head", "blk")),
            P("blk", "head"),
            P("blk", "head"),
            P("head", "blk"),
        ),
        check_vma=False,
    )
```

profile of v0, /device:TPU:0, one launch (start us, length us, event | category | flops | bytes accessed | tf_op | source)
XLA Modules:
  0.0 1761.1 jit_solution(9921900207818118351)
XLA Ops:
  10.7 22.2 %all-gather = bf16[8,1,256]{2,1,0:T(2,128)(2,1)S(1)} all-gather(bf16[1,1,256]{2,1,0:T(2,128)(2,1)S(1)} %reshape.657), channel_id=1, replica_groups=mesh['head'=4,'blk'=8] {'blk'}, dimensions={0}, use_global_device_ids=true | all-gather | bytes 4608 | tf_op jit(solution)/shard_map/all_gather | solution.py:118
  36.7 17.2 all-reduce.15
  58.3 18.9 %all-gather.17.cloned.1.call-done = bf16[2048,256]{1,0:T(8,128)(2,1)} async-done(((bf16[256,256]{1,0:T(8,128)(2,1)}), bf16[2048,256]{1,0:T(8,128)(2,1)}) %all-gather.17.cloned.1.call-update) | async-done | bytes 1048592 | tf_op jit(solution)/shard_map/all_gather | solution.py:120
  81.6 36.7 %all-gather.19.cloned.1.call-done = bf16[2048,256]{1,0:T(8,128)(2,1)} async-done(((bf16[256,256]{1,0:T(8,128)(2,1)}), bf16[2048,256]{1,0:T(8,128)(2,1)}) %all-gather.19.cloned.1.call-update) | async-done | bytes 1048592 | tf_op jit(solution)/shard_map/all_gather | solution.py:121
  125.3 43.0 %all-gather.23.cloned.1.call-done = bf16[2048,512]{1,0:T(8,128)(2,1)} async-done(((bf16[256,512]{1,0:T(8,128)(2,1)}), bf16[2048,512]{1,0:T(8,128)(2,1)}) %all-gather.23.cloned.1.call-update) | async-done | bytes 2097168 | tf_op jit(solution)/shard_map/all_gather | solution.py:119
  173.2 69.6 %all-gather.21.cloned.1.call-done = bf16[2,4096,256]{2,1,0:T(8,128)(2,1)} async-done(((bf16[2,512,256]{2,1,0:T(8,128)(2,1)}), bf16[2,4096,256]{2,1,0:T(8,128)(2,1)}) %all-gather.21.cloned.1.call-update) | async-done | bytes 4194320 | tf_op jit(solution)/shard_map/all_gather | solution.py:211
  251.3 15.1 fusion.23
  270.6 14.2 fusion.26
  284.8 15.3 fusion.112
  305.5 17.8 %all-gather.1 = bf16[8,1,256]{2,1,0:T(2,128)(2,1)S(1)} all-gather(bf16[1,1,256]{2,1,0:T(2,128)(2,1)S(1)} %reshape.659), channel_id=1, replica_groups=mesh['head'=4,'blk'=8] {'blk'}, dimensions={0}, use_global_device_ids=true | all-gather | bytes 4608 | tf_op jit(solution)/shard_map/all_gather | solution.py:125
  323.3 11.2 reduce-scatter.12.cloned.1.call-done
  340.0 96.0 %all-gather.29.cloned.1.call-done = bf16[2048,1536]{1,0:T(8,128)(2,1)} async-done(((bf16[256,1536]{1,0:T(8,128)(2,1)}), bf16[2048,1536]{1,0:T(8,128)(2,1)}) %all-gather.29.cloned.1.call-update) | async-done | bytes 6291472 | tf_op jit(solution)/shard_map/all_gather | solution.py:126
  436.0 23.0 %all-gather.27.cloned.1.call-done = bf16[512,2048]{1,0:T(8,128)(2,1)} async-done(((bf16[128,2048]{1,0:T(8,128)(2,1)}), bf16[512,2048]{1,0:T(8,128)(2,1)}) %all-gather.27.cloned.1.call-update) | async-done | bytes 2097168 | tf_op jit(solution)/shard_map/all_gather | solution.py:224
  459.0 8.5 fusion.115
  467.5 92.8 %all-gather.31.cloned.1.call-done = bf16[2048,1536]{1,0:T(8,128)(2,1)} async-done(((bf16[256,1536]{1,0:T(8,128)(2,1)}), bf16[2048,1536]{1,0:T(8,128)(2,1)}) %all-gather.31.cloned.1.call-update) | async-done | bytes 6291472 | tf_op jit(solution)/shard_map/all_gather | solution.py:127
  560.3 8.5 fusion.116
  568.8 13.9 all-gather.35.cloned.1.call-done
  582.8 102.1 %all-gather.33.cloned.1.call-done = bf16[1536,2048]{1,0:T(8,128)(2,1)} async-done(((bf16[1536,256]{1,0:T(8,128)(2,1)}), bf16[1536,2048]{1,0:T(8,128)(2,1)}) %all-gather.33.cloned.1.call-update) | async-done | bytes 6291472 | tf_op jit(solution)/shard_map/all_gather | solution.py:128
  684.8 11.0 multiply_convert_fusion
  695.9 6.7 fusion.117
  707.4 29.7 %reduce-scatter.16.cloned.1.call-done = bf16[128,2048]{1,0:T(8,128)(2,1)} async-done(((bf16[512,2048]{1,0:T(8,128)(2,1)}), bf16[128,2048]{1,0:T(8,128)(2,1)}) %reduce-scatter.16.cloned.1.call-update) | async-done | bytes 524304 | tf_op jit(solution)/shard_map/reduce_scatter | solution.py:248
  743.7 20.8 %all-gather.37.cloned.1.call-done = bf16[512,2048]{1,0:T(8,128)(2,1)} async-done(((bf16[128,2048]{1,0:T(8,128)(2,1)}), bf16[512,2048]{1,0:T(8,128)(2,1)}) %all-gather.37.cloned.1.call-update) | async-done | bytes 2097168 | tf_op jit(solution)/shard_map/all_gather | solution.py:257
  769.7 279.6 %while.21 = (s32[]{:T(128)}, f32[512,2,2,128]{3,0,2,1:T(8,128)}, bf16[2,512,256]{1,2,0:T(8,128)(2,1)}, f32[2,512,256]{1,2,0:T(8,128)}, s32[]{:T(128)}, /*index=5...) while((s32[]{:T(128)}, f32[512,2,2,128]{3,0,2,1:T(8,128)}, ...), condition=%wide.region_17.18_spmd.clone, body=%wide.region_15.17_spmd.clone.sunk | while | flops 1353261568 | bytes 40444412 | solution.py:308
  784.3 12.9 collective-permute-done.1
  799.3 8.4 collective-permute-done
  821.8 13.6 collective-permute-done.1
  837.5 7.5 collective-permute-done
  857.9 14.7 collective-permute-done.1
  874.8 6.5 collective-permute-done
  894.2 14.7 collective-permute-done.1
  929.7 14.7 collective-permute-done.1
  964.2 14.7 collective-permute-done.1
  997.8 14.1 collective-permute-done.1
  1030.4 13.2 collective-permute-done.1
  1074.0 8.2 convolution_convert_fusion.5
  1082.3 6.8 convolution_convert_fusion.1
  1089.2 6.8 convolution_convert_fusion.2
  1097.6 6.8 convolution_convert_fusion
  1108.2 6.3 all-reduce.16
  1114.9 17.2 all-reduce.14
  1134.9 45.9 %reduce-scatter.24.cloned.1.call-done = bf16[256,256]{1,0:T(8,128)(2,1)} async-done(((bf16[2048,256]{1,0:T(8,128)(2,1)}), bf16[256,256]{1,0:T(8,128)(2,1)}) %reduce-scatter.24.cloned.1.call-update) | async-done | bytes 131088 | tf_op jit(solution)/shard_map/reduce_scatter | solution.py:369
  1182.4 69.0 %reduce-scatter.26.cloned.1.call-done = bf16[512,256]{1,0:T(8,128)(2,1)} async-done(((bf16[512,2048]{1,0:T(8,128)(2,1)}), bf16[512,256]{1,0:T(8,128)(2,1)}) %reduce-scatter.26.cloned.1.call-update) | async-done | bytes 262160 | tf_op jit(solution)/shard_map/reduce_scatter | solution.py:378
  1253.2 68.3 %reduce-scatter.20.cloned.1.call-done = bf16[256,512]{1,0:T(8,128)(2,1)} async-done(((bf16[2048,512]{1,0:T(8,128)(2,1)}), bf16[256,512]{1,0:T(8,128)(2,1)}) %reduce-scatter.20.cloned.1.call-update) | async-done | bytes 262160 | tf_op jit(solution)/shard_map/reduce_scatter | solution.py:363
  1323.3 31.2 %reduce-scatter.18.cloned.1.call-done = bf16[128,2048]{1,0:T(8,128)(2,1)} async-done(((bf16[512,2048]{1,0:T(8,128)(2,1)}), bf16[128,2048]{1,0:T(8,128)(2,1)}) %reduce-scatter.18.cloned.1.call-update) | async-done | bytes 524304 | tf_op jit(solution)/shard_map/reduce_scatter | solution.py:340
  1355.8 32.7 %reduce-scatter.14.cloned.1.call-done = bf16[128,2048]{1,0:T(8,128)(2,1)} async-done(((bf16[512,2048]{1,0:T(8,128)(2,1)}), bf16[128,2048]{1,0:T(8,128)(2,1)}) %reduce-scatter.14.cloned.1.call-update) | async-done | bytes 524304 | tf_op jit(solution)/shard_map/reduce_scatter | solution.py:232
  1391.7 118.4 %reduce-scatter.30.cloned.1.call-done = bf16[256,1536]{1,0:T(8,128)(2,1)} async-done(((bf16[2048,1536]{1,0:T(8,128)(2,1)}), bf16[256,1536]{1,0:T(8,128)(2,1)}) %reduce-scatter.30.cloned.1.call-update) | async-done | bytes 786448 | tf_op jit(solution)/shard_map/reduce_scatter | solution.py:387
  1512.5 118.3 %reduce-scatter.28.cloned.1.call-done = bf16[256,1536]{1,0:T(8,128)(2,1)} async-done(((bf16[2048,1536]{1,0:T(8,128)(2,1)}), bf16[256,1536]{1,0:T(8,128)(2,1)}) %reduce-scatter.28.cloned.1.call-update) | async-done | bytes 786448 | tf_op jit(solution)/shard_map/reduce_scatter | solution.py:384
  1633.2 118.8 %reduce-scatter.32.cloned.1.call-done = bf16[1536,256]{1,0:T(8,128)(2,1)} async-done(((bf16[1536,2048]{1,0:T(8,128)(2,1)}), bf16[1536,256]{1,0:T(8,128)(2,1)}) %reduce-scatter.32.cloned.1.call-update) | async-done | bytes 786448 | tf_op jit(solution)/shard_map/reduce_scatter | solution.py:390
  (411 shorter events, 257.9 us)
Async XLA Ops:
  7.2 49.0 %all-gather.15.cloned.1.call-start = ((), (), s32[]{:S(2)}) async-start(), calls=%async_computation.11 | async-start | bytes 2621440 | tf_op jit(solution)/shard_map/all_gather | solution.py:161
  7.9 69.3 %all-gather.17.cloned.1.call-start = ((), (), s32[]{:S(2)}) async-start(), calls=%async_computation.12 | async-start | bytes 1179648 | tf_op jit(solution)/shard_map/all_gather | solution.py:120
  8.7 109.6 %all-gather.19.cloned.1.call-start = ((), (), s32[]{:S(2)}) async-start(), calls=%async_computation.13 | async-start | bytes 1179648 | tf_op jit(solution)/shard_map/all_gather | solution.py:121
  9.4 158.9 %all-gather.23.cloned.1.call-start = ((), (), s32[]{:S(2)}) async-start(), calls=%async_computation.15 | async-start | bytes 2359296 | tf_op jit(solution)/shard_map/all_gather | solution.py:119
  10.0 232.9 %all-gather.21.cloned.1.call-start = ((), (), s32[]{:S(2)}) async-start(), calls=%async_computation.14 | async-start | bytes 4718592 | tf_op jit(solution)/shard_map/all_gather | solution.py:211
  32.9 135.4 %copy-start.27 = (f32[8,1,256]{2,1,0:T(1,128)}, f32[8,1,256]{2,1,0:T(1,128)S(1)}, u32[]{:S(2)}) copy-start(f32[8,1,256]{2,1,0:T(1,128)S(1)} %convert_element_type.323) | copy-start | bytes 24580
  121.1 179.0 %all-gather.25.cloned.1.call-start = ((), (), s32[]{:S(2)}) async-start(), calls=%async_computation.16 | async-start | bytes 2359296 | tf_op jit(solution)/shard_map/all_gather | solution.py:124
  121.7 212.8 %reduce-scatter.12.cloned.1.call-start = ((), (), s32[]{:S(2)}) async-start(), calls=%async_computation.17 | async-start | bytes 2621440 | tf_op jit(solution)/shard_map/reduce_scatter | solution.py:218
  304.6 131.3 %all-gather.29.cloned.1.call-start = ((), (), s32[]{:S(2)}) async-start(), calls=%async_computation.19 | async-start | bytes 7077888 | tf_op jit(solution)/shard_map/all_gather | solution.py:126
  305.4 153.6 %all-gather.27.cloned.1.call-start = ((), (), s32[]{:S(2)}) async-start(), calls=%async_computation.18 | async-start | bytes 2621440 | tf_op jit(solution)/shard_map/all_gather | solution.py:224
  335.8 403.7 %copy-start.36 = (f32[128]{0:T(128)}, f32[128]{0:T(128)S(1)}, u32[]{:S(2)}) copy-start(f32[128]{0:T(128)S(1)} %fusion.97) | copy-start | bytes 1540
  337.8 222.5 %all-gather.31.cloned.1.call-start = ((), (), s32[]{:S(2)}) async-start(), calls=%async_computation.20 | async-start | bytes 7077888 | tf_op jit(solution)/shard_map/all_gather | solution.py:127
  338.4 244.3 %all-gather.35.cloned.1.call-start = ((), (), s32[]{:S(2)}) async-start(), calls=%async_computation.23 | async-start | bytes 2621440 | tf_op jit(solution)/shard_map/all_gather | solution.py:239
  339.2 345.6 %all-gather.33.cloned.1.call-start = ((), (), s32[]{:S(2)}) async-start(), calls=%async_computation.21 | async-start | bytes 7077888 | tf_op jit(solution)/shard_map/all_gather | solution.py:128
  339.7 397.4 %reduce-scatter.16.cloned.1.call-start = ((), (), s32[]{:S(2)}) async-start(), calls=%async_computation.24 | async-start | bytes 2621440 | tf_op jit(solution)/shard_map/reduce_scatter | solution.py:248
  707.4 57.1 %all-gather.37.cloned.1.call-start = ((), (), s32[]{:S(2)}) async-start(), calls=%async_computation.25 | async-start | bytes 2621440 | tf_op jit(solution)/shard_map/all_gather | solution.py:257
  741.8 391.5 %reduce-scatter.22.cloned.1.call-start = ((), (), s32[]{:S(2)}) async-start(), calls=%async_computation.28 | async-start | bytes 1179648 | tf_op jit(solution)/shard_map/reduce_scatter | solution.py:366
  779.4 17.8 %collective-permute-start.1 = (bf16[2,512,256]{1,2,0:T(8,128)(2,1)}, bf16[2,512,256]{1,2,0:T(8,128)(2,1)}, u32[]{:S(2)}, u32[]{:S(2)}) collective-permute-start(bf16[2,512,256]{1,2,0:T(8,128)(2,1)} %fusion.201), channel_id=1, source_target_pairs={{0,1},{1,2},{2,3},{3,4},{4,5},{5,6},{6,7},{7,0},{8,9},{9,10},{10,1... | collective-permute-start | bytes 1572872 | tf_op jit(solution)/shard_map/while/body/eval_jaxpr/ppermute | solution.py:17
  780.9 26.9 %collective-permute-start = (bf16[2,512,256]{1,2,0:T(8,128)(2,1)S(1)}, bf16[2,512,256]{1,2,0:T(8,128)(2,1)}, u32[]{:S(2)}, u32[]{:S(2)}) collective-permute-start(bf16[2,512,256]{1,2,0:T(8,128)(2,1)S(1)} %copy.123), channel_id=1, source_target_pairs={{0,1},{1,2},{2,3},{3,4},{4,5},{5,6},{6,7},{7,0},{8,9},{9,10},{10,1... | collective-permute-start | bytes 1572872 | tf_op jit(solution)/shard_map/while/body/eval_jaxpr/ppermute | solution.py:17
  817.5 17.9 %collective-permute-start.1 = (bf16[2,512,256]{1,2,0:T(8,128)(2,1)}, bf16[2,512,256]{1,2,0:T(8,128)(2,1)}, u32[]{:S(2)}, u32[]{:S(2)}) collective-permute-start(bf16[2,512,256]{1,2,0:T(8,128)(2,1)} %fusion.201), channel_id=1, source_target_pairs={{0,1},{1,2},{2,3},{3,4},{4,5},{5,6},{6,7},{7,0},{8,9},{9,10},{10,1... | collective-permute-start | bytes 1572872 | tf_op jit(solution)/shard_map/while/body/eval_jaxpr/ppermute | solution.py:17
  817.5 27.5 %collective-permute-start = (bf16[2,512,256]{1,2,0:T(8,128)(2,1)S(1)}, bf16[2,512,256]{1,2,0:T(8,128)(2,1)}, u32[]{:S(2)}, u32[]{:S(2)}) collective-permute-start(bf16[2,512,256]{1,2,0:T(8,128)(2,1)S(1)} %copy.123), channel_id=1, source_target_pairs={{0,1},{1,2},{2,3},{3,4},{4,5},{5,6},{6,7},{7,0},{8,9},{9,10},{10,1... | collective-permute-start | bytes 1572872 | tf_op jit(solution)/shard_map/while/body/eval_jaxpr/ppermute | solution.py:17
  854.8 17.9 %collective-permute-start.1 = (bf16[2,512,256]{1,2,0:T(8,128)(2,1)}, bf16[2,512,256]{1,2,0:T(8,128)(2,1)}, u32[]{:S(2)}, u32[]{:S(2)}) collective-permute-start(bf16[2,512,256]{1,2,0:T(8,128)(2,1)} %fusion.201), channel_id=1, source_target_pairs={{0,1},{1,2},{2,3},{3,4},{4,5},{5,6},{6,7},{7,0},{8,9},{9,10},{10,1... | collective-permute-start | bytes 1572872 | tf_op jit(solution)/shard_map/while/body/eval_jaxpr/ppermute | solution.py:17
  854.8 26.6 %collective-permute-start = (bf16[2,512,256]{1,2,0:T(8,128)(2,1)S(1)}, bf16[2,512,256]{1,2,0:T(8,128)(2,1)}, u32[]{:S(2)}, u32[]{:S(2)}) collective-permute-start(bf16[2,512,256]{1,2,0:T(8,128)(2,1)S(1)} %copy.123), channel_id=1, source_target_pairs={{0,1},{1,2},{2,3},{3,4},{4,5},{5,6},{6,7},{7,0},{8,9},{9,10},{10,1... | collective-permute-start | bytes 1572872 | tf_op jit(solution)/shard_map/while/body/eval_jaxpr/ppermute | solution.py:17
  891.1 17.9 %collective-permute-start.1 = (bf16[2,512,256]{1,2,0:T(8,128)(2,1)}, bf16[2,512,256]{1,2,0:T(8,128)(2,1)}, u32[]{:S(2)}, u32[]{:S(2)}) collective-permute-start(bf16[2,512,256]{1,2,0:T(8,128)(2,1)} %fusion.201), channel_id=1, source_target_pairs={{0,1},{1,2},{2,3},{3,4},{4,5},{5,6},{6,7},{7,0},{8,9},{9,10},{10,1... | collective-permute-start | bytes 1572872 | tf_op jit(solution)/shard_map/while/body/eval_jaxpr/ppermute | solution.py:17
  891.1 25.7 %collective-permute-start = (bf16[2,512,256]{1,2,0:T(8,128)(2,1)S(1)}, bf16[2,512,256]{1,2,0:T(8,128)(2,1)}, u32[]{:S(2)}, u32[]{:S(2)}) collective-permute-start(bf16[2,512,256]{1,2,0:T(8,128)(2,1)S(1)} %copy.123), channel_id=1, source_target_pairs={{0,1},{1,2},{2,3},{3,4},{4,5},{5,6},{6,7},{7,0},{8,9},{9,10},{10,1... | collective-permute-start | bytes 1572872 | tf_op jit(solution)/shard_map/while/body/eval_jaxpr/ppermute | solution.py:17
  926.5 17.9 %collective-permute-start.1 = (bf16[2,512,256]{1,2,0:T(8,128)(2,1)}, bf16[2,512,256]{1,2,0:T(8,128)(2,1)}, u32[]{:S(2)}, u32[]{:S(2)}) collective-permute-start(bf16[2,512,256]{1,2,0:T(8,128)(2,1)} %fusion.201), channel_id=1, source_target_pairs={{0,1},{1,2},{2,3},{3,4},{4,5},{5,6},{6,7},{7,0},{8,9},{9,10},{10,1... | collective-permute-start | bytes 1572872 | tf_op jit(solution)/shard_map/while/body/eval_jaxpr/ppermute | solution.py:17
  926.5 24.7 %collective-permute-start = (bf16[2,512,256]{1,2,0:T(8,128)(2,1)S(1)}, bf16[2,512,256]{1,2,0:T(8,128)(2,1)}, u32[]{:S(2)}, u32[]{:S(2)}) collective-permute-start(bf16[2,512,256]{1,2,0:T(8,128)(2,1)S(1)} %copy.123), channel_id=1, source_target_pairs={{0,1},{1,2},{2,3},{3,4},{4,5},{5,6},{6,7},{7,0},{8,9},{9,10},{10,1... | collective-permute-start | bytes 1572872 | tf_op jit(solution)/shard_map/while/body/eval_jaxpr/ppermute | solution.py:17
  961.0 17.9 %collective-permute-start.1 = (bf16[2,512,256]{1,2,0:T(8,128)(2,1)}, bf16[2,512,256]{1,2,0:T(8,128)(2,1)}, u32[]{:S(2)}, u32[]{:S(2)}) collective-permute-start(bf16[2,512,256]{1,2,0:T(8,128)(2,1)} %fusion.201), channel_id=1, source_target_pairs={{0,1},{1,2},{2,3},{3,4},{4,5},{5,6},{6,7},{7,0},{8,9},{9,10},{10,1... | collective-permute-start | bytes 1572872 | tf_op jit(solution)/shard_map/while/body/eval_jaxpr/ppermute | solution.py:17
  961.0 23.8 %collective-permute-start = (bf16[2,512,256]{1,2,0:T(8,128)(2,1)S(1)}, bf16[2,512,256]{1,2,0:T(8,128)(2,1)}, u32[]{:S(2)}, u32[]{:S(2)}) collective-permute-start(bf16[2,512,256]{1,2,0:T(8,128)(2,1)S(1)} %copy.123), channel_id=1, source_target_pairs={{0,1},{1,2},{2,3},{3,4},{4,5},{5,6},{6,7},{7,0},{8,9},{9,10},{10,1... | collective-permute-start | bytes 1572872 | tf_op jit(solution)/shard_map/while/body/eval_jaxpr/ppermute | solution.py:17
  994.6 17.3 collective-permute-start.1
  994.6 22.9 %collective-permute-start = (bf16[2,512,256]{1,2,0:T(8,128)(2,1)S(1)}, bf16[2,512,256]{1,2,0:T(8,128)(2,1)}, u32[]{:S(2)}, u32[]{:S(2)}) collective-permute-start(bf16[2,512,256]{1,2,0:T(8,128)(2,1)S(1)} %copy.123), channel_id=1, source_target_pairs={{0,1},{1,2},{2,3},{3,4},{4,5},{5,6},{6,7},{7,0},{8,9},{9,10},{10,1... | collective-permute-start | bytes 1572872 | tf_op jit(solution)/shard_map/while/body/eval_jaxpr/ppermute | solution.py:17
  1027.3 16.4 collective-permute-start.1
  1027.3 22.0 %collective-permute-start = (bf16[2,512,256]{1,2,0:T(8,128)(2,1)S(1)}, bf16[2,512,256]{1,2,0:T(8,128)(2,1)}, u32[]{:S(2)}, u32[]{:S(2)}) collective-permute-start(bf16[2,512,256]{1,2,0:T(8,128)(2,1)S(1)} %copy.123), channel_id=1, source_target_pairs={{0,1},{1,2},{2,3},{3,4},{4,5},{5,6},{6,7},{7,0},{8,9},{9,10},{10,1... | collective-permute-start | bytes 1572872 | tf_op jit(solution)/shard_map/while/body/eval_jaxpr/ppermute | solution.py:17
  1055.0 125.8 %reduce-scatter.24.cloned.1.call-start = ((), (), s32[]{:S(2)}) async-start(), calls=%async_computation.29 | async-start | bytes 1179648 | tf_op jit(solution)/shard_map/reduce_scatter | solution.py:369
  1057.1 194.3 %reduce-scatter.26.cloned.1.call-start = ((), (), s32[]{:S(2)}) async-start(), calls=%async_computation.30 | async-start | bytes 2359296 | tf_op jit(solution)/shard_map/reduce_scatter | solution.py:378
  1061.6 259.9 %reduce-scatter.20.cloned.1.call-start = ((), (), s32[]{:S(2)}) async-start(), calls=%async_computation.27 | async-start | bytes 2359296 | tf_op jit(solution)/shard_map/reduce_scatter | solution.py:363
  1067.1 287.4 %reduce-scatter.18.cloned.1.call-start = ((), (), s32[]{:S(2)}) async-start(), calls=%async_computation.26 | async-start | bytes 2621440 | tf_op jit(solution)/shard_map/reduce_scatter | solution.py:340
  1074.0 314.5 %reduce-scatter.14.cloned.1.call-start = ((), (), s32[]{:S(2)}) async-start(), calls=%async_computation.22 | async-start | bytes 2621440 | tf_op jit(solution)/shard_map/reduce_scatter | solution.py:232
  1082.2 427.8 %reduce-scatter.30.cloned.1.call-start = ((), (), s32[]{:S(2)}) async-start(), calls=%async_computation.32 | async-start | bytes 7077888 | tf_op jit(solution)/shard_map/reduce_scatter | solution.py:387
  1089.2 541.6 %reduce-scatter.28.cloned.1.call-start = ((), (), s32[]{:S(2)}) async-start(), calls=%async_computation.31 | async-start | bytes 7077888 | tf_op jit(solution)/shard_map/reduce_scatter | solution.py:384
  1096.0 655.9 %reduce-scatter.32.cloned.1.call-start = ((), (), s32[]{:S(2)}) async-start(), calls=%async_computation.33 | async-start | bytes 7077888 | tf_op jit(solution)/shard_map/reduce_scatter | solution.py:390
  1104.4 250.1 %copy-start.3 = (bf16[128,2048]{1,0:T(8,128)(2,1)S(1)}, bf16[128,2048]{1,0:T(8,128)(2,1)}, u32[]{:S(2)}) copy-start(bf16[128,2048]{1,0:T(8,128)(2,1)} %param.17) | copy-start | bytes 1572868
  1105.0 250.8 %copy-start.44 = (f32[128]{0:T(128)S(1)}, f32[128]{0:T(128)}, u32[]{:S(2)}) copy-start(f32[128]{0:T(128)} %get-tuple-element.451) | copy-start | bytes 1540
  1105.0 283.4 %copy-start.7 = (bf16[128,2048]{1,0:T(8,128)(2,1)S(1)}, bf16[128,2048]{1,0:T(8,128)(2,1)}, u32[]{:S(2)}) copy-start(bf16[128,2048]{1,0:T(8,128)(2,1)} %reduce-scatter.12.cloned.1.call-done) | copy-start | bytes 1572868
  1105.0 283.4 %copy-start.14 = (bf16[128,2048]{1,0:T(8,128)(2,1)S(1)}, bf16[128,2048]{1,0:T(8,128)(2,1)}, u32[]{:S(2)}) copy-start(bf16[128,2048]{1,0:T(8,128)(2,1)} %reduce-scatter.16.cloned.1.call-done) | copy-start | bytes 1572868
  1105.0 283.4 %copy-start.16 = (bf16[128,2048]{1,0:T(8,128)(2,1)S(1)}, bf16[128,2048]{1,0:T(8,128)(2,1)}, u32[]{:S(2)}) copy-start(bf16[128,2048]{1,0:T(8,128)(2,1)} %param.18) | copy-start | bytes 1572868
  1105.0 283.4 %copy-start.37 = (f32[128]{0:T(128)S(1)}, f32[128]{0:T(128)}, u32[]{:S(2)}) copy-start(f32[128]{0:T(128)} %copy-done.36) | copy-start | bytes 1540
  1105.0 283.4 %copy-start.46 = (f32[128]{0:T(128)S(1)}, f32[128]{0:T(128)}, u32[]{:S(2)}) copy-start(f32[128]{0:T(128)} %copy-done.45) | copy-start | bytes 1540
  (63 other events, 646.4 us)
Sparse Core Ops, SparseCore 0:
  9.6 25.2 all-gather.14
  37.0 40.1 all-gather.16
  79.3 38.8 all-gather.18
  120.3 48.0 all-gather.22
  170.9 71.8 all-gather.20
  244.7 49.3 all-gather.24
  304.7 29.6 reduce-scatter.11
  336.9 99.0 all-gather.28
  438.2 20.7 all-gather.26
  461.2 99.0 all-gather.30
  561.9 20.7 all-gather.34
  584.9 99.9 all-gather.32
  707.5 29.6 reduce-scatter.15
  741.9 22.5 all-gather.36
  1055.1 59.4 reduce-scatter.21
  1118.3 62.4 reduce-scatter.23
  1184.2 67.1 reduce-scatter.25
  1254.8 66.6 reduce-scatter.19
  1324.0 30.4 reduce-scatter.17
  1357.0 31.3 reduce-scatter.13
  1392.1 117.9 reduce-scatter.29
  1513.6 117.0 reduce-scatter.27
  1634.4 117.5 reduce-scatter.31
where the time goes:
time: 1770 us; the launch traced here: 1760 us
  waiting for transfers between devices  1320 us (75%)
  matrix products  205 us (12%)
  other arithmetic  89.5 us (5%)
  blocking collectives  80.8 us (5%)
  local copies, waits for them, and re-layouts  38 us (2%)
  between operations  18.2 us (1%)
    ppermute x16, waiting for transfers between devices, shifted(): return lax.ppermute(value, axis, pairs)  156 us
    reduce_scatter x1, waiting for transfers between devices, shards(): lax.psum_scatter(down_wgrad.astype(jnp.bfloat16), 'blk', scatter_dimensio...  119 us
    reduce_scatter x1, waiting for transfers between devices, shards(): lax.psum_scatter(up_wgrad.astype(jnp.bfloat16), 'blk', scatter_dimension=...  118 us
    reduce_scatter x1, waiting for transfers between devices, shards(): lax.psum_scatter(gate_wgrad.astype(jnp.bfloat16), 'blk', scatter_dimensio...  118 us
    all_gather x1, waiting for transfers between devices, shards(): lax.all_gather(down_weight, 'blk', axis=1, tiled=True)  102 us
    all_gather x1, waiting for transfers between devices, shards(): lax.all_gather(gate_weight, 'blk', axis=0, tiled=True)  96 us
    all_gather x1, waiting for transfers between devices, shards(): lax.all_gather(up_weight, 'blk', axis=0, tiled=True)  92.8 us
    all_gather x1, waiting for transfers between devices, shards(): key_piece = lax.all_gather(kv_pair, 'blk', axis=1, tiled=True)  69.6 us
  transfers between devices with their start and end apart: 39, of which 36 were waited for; matrix products, arithmetic and copies ran while one was open for 12% of the time, Pallas kernels for 0%

commit v1 on v0

v1 whole, which is shorter than its diff:
```python
import functools
import math

import jax
import jax.numpy as jnp
from jax import lax
from jax.experimental import pallas as pl
from jax.experimental.pallas import tpu as pltpu
from jax.sharding import Mesh
from jax.sharding import PartitionSpec as P

HEAD_SIZE = 128
KEY_VALUE_HEADS = 8
EPSILON = 1e-06
ROPE_BASE = 1000000.0
F32 = jnp.float32
BF16 = jnp.bfloat16
SWAP = [(0, 1), (1, 0)]
PAIRS_OF_ROWS = (((0,), (0,)), ((), ()))
PAIRS_OF_COLS = (((1,), (1,)), ((), ()))
VMEM = pltpu.MemorySpace.VMEM
SMEM = pltpu.MemorySpace.SMEM


def matmul(left, right):
    return jnp.dot(left, right, preferred_element_type=F32)


def contract_rows(left, right):
    return lax.dot_general(left, right, PAIRS_OF_ROWS, preferred_element_type=F32)


def contract_cols(left, right):
    return lax.dot_general(left, right, PAIRS_OF_COLS, preferred_element_type=F32)


def swap(value, axis):
    return lax.ppermute(value, axis, SWAP)


def attend_kernel(off_ref, tile_ref, q_ref, kv_ref, start_ref, out_ref, inv_ref, acc_ref):
    half = 128
    lane = lax.broadcasted_iota(jnp.int32, (256, 256), 1)
    row = lax.broadcasted_iota(jnp.int32, (256, 256), 0) % half
    ones = jnp.ones((256, HEAD_SIZE), BF16)

    def tile(index, unused):
        first = pl.multiple_of(index * half, half)
        rows = pl.ds(first, half)
        queries = jnp.concatenate([q_ref[rows, :HEAD_SIZE], q_ref[rows, HEAD_SIZE:]], axis=0)
        start = start_ref[rows, :]
        start = jnp.concatenate([start, start], axis=1)
        start = jnp.concatenate([start, start], axis=0)
        places = tile_ref[0, index] * half + row
        acc_ref[...] = jnp.zeros_like(acc_ref)

        def step(block, unused_step):
            low = pl.ds(pl.multiple_of(off_ref[2 * block], half), half)
            high = pl.ds(pl.multiple_of(off_ref[2 * block + 1], half), half)
            keys = jnp.concatenate([kv_ref[low, :HEAD_SIZE], kv_ref[high, :HEAD_SIZE]], axis=0)
            values = jnp.concatenate([kv_ref[low, HEAD_SIZE:], kv_ref[high, HEAD_SIZE:]], axis=0)
            scores = contract_cols(queries, keys)
            natural = block * 256 + lane
            allowed = (natural <= places) & (natural >= start)
            weights = jnp.where(allowed, jnp.exp(scores), 0.0).astype(BF16)
            acc_ref[...] += matmul(weights, jnp.concatenate([values, ones], axis=1))
            return unused_step

        lax.fori_loop(tile_ref[1, index], tile_ref[2, index] + 1, step, 0)
        inverse = 1.0 / acc_ref[:, HEAD_SIZE:]
        attended = (acc_ref[:, :HEAD_SIZE] * inverse).astype(BF16)
        out_ref[rows, :HEAD_SIZE] = attended[:half]
        out_ref[rows, HEAD_SIZE:] = attended[half:]
        inv_ref[index, 0:1, :] = jnp.transpose(inverse[:half])[0:1, :]
        inv_ref[index, 1:2, :] = jnp.transpose(inverse[half:])[0:1, :]
        return unused

    lax.fori_loop(0, q_ref.shape[0] // half, tile, 0)


def attend_back_kernel(
    off_ref, tile_ref, q_ref, kv_ref, start_ref, inv_ref, out_ref, grad_ref, dq_ref, dkv_ref, dk_ref, dv_ref, acc_ref
):
    half = 128
    key_row = lax.broadcasted_iota(jnp.int32, (256, 256), 0)
    query_lane = lax.broadcasted_iota(jnp.int32, (1, 256), 1) % half

    def clear(index, unused):
        rows = pl.ds(pl.multiple_of(index * 256, 256), 256)
        dk_ref[rows, :] = jnp.zeros((256, HEAD_SIZE), F32)
        dv_ref[rows, :] = jnp.zeros((256, HEAD_SIZE), F32)
        return unused

    lax.fori_loop(0, dk_ref.shape[0] // 256, clear, 0)

    def tile(index, unused):
        first = pl.multiple_of(index * half, half)
        rows = pl.ds(first, half)

        def both(ref):
            return jnp.concatenate([ref[rows, :HEAD_SIZE], ref[rows, HEAD_SIZE:]], axis=0)

        def along(ref):
            return jnp.concatenate([ref[index, 0:1, :], ref[index, 1:2, :]], axis=1)

        queries = both(q_ref)
        grads = both(grad_ref)
        products = both(out_ref).astype(F32) * grads.astype(F32)
        deltas = jnp.sum(jnp.transpose(products), axis=0, keepdims=True)
        inverse = along(inv_ref)
        start = along(start_ref)
        places = tile_ref[0, index] * half + query_lane
        acc_ref[...] = jnp.zeros_like(acc_ref)

        def step(block, unused_step):
            low = pl.ds(pl.multiple_of(off_ref[2 * block], half), half)
            high = pl.ds(pl.multiple_of(off_ref[2 * block + 1], half), half)
            keys = jnp.concatenate([kv_ref[low, :HEAD_SIZE], kv_ref[high, :HEAD_SIZE]], axis=0)
            values = jnp.concatenate([kv_ref[low, HEAD_SIZE:], kv_ref[high, HEAD_SIZE:]], axis=0)
            scores = contract_cols(keys, queries)
            natural = block * 256 + key_row
            allowed = (natural <= places) & (natural >= start)
            probs = jnp.where(allowed, jnp.exp(scores) * inverse, 0.0)
            prob_grad = contract_cols(values, grads)
            score_grad = (probs * (prob_grad - deltas)).astype(BF16)
            value_part = matmul(probs.astype(BF16), grads)
            key_part = matmul(score_grad, queries)
            dv_ref[low, :] += value_part[:half]
            dv_ref[high, :] += value_part[half:]
            dk_ref[low, :] += key_part[:half]
            dk_ref[high, :] += key_part[half:]
            acc_ref[...] += contract_rows(score_grad, keys)
            return unused_step

        lax.fori_loop(tile_ref[1, index], tile_ref[2, index] + 1, step, 0)
        query_grad = acc_ref[...].astype(BF16)
        dq_ref[rows, :HEAD_SIZE] = query_grad[:half]
        dq_ref[rows, HEAD_SIZE:] = query_grad[half:]
        return unused

    lax.fori_loop(0, q_ref.shape[0] // half, tile, 0)

    def store(index, unused):
        rows = pl.ds(pl.multiple_of(index * 256, 256), 256)
        dkv_ref[rows, :HEAD_SIZE] = dk_ref[rows, :].astype(BF16)
        dkv_ref[rows, HEAD_SIZE:] = dv_ref[rows, :].astype(BF16)
        return unused

    lax.fori_loop(0, dk_ref.shape[0] // 256, store, 0)


def attend(offsets, tiles, queries, key_values, start_cols):
    rows, width = queries.shape
    keys = key_values.shape[0]
    return pl.pallas_call(
        attend_kernel,
        name="attend",
        out_shape=(
            jax.ShapeDtypeStruct((rows, width), BF16),
            jax.ShapeDtypeStruct((rows // 128, 2, 128), F32),
        ),
        in_specs=[pl.BlockSpec(memory_space=SMEM)] * 2 + [pl.BlockSpec(memory_space=VMEM)] * 3,
        out_specs=[pl.BlockSpec(memory_space=VMEM)] * 2,
        scratch_shapes=[pltpu.VMEM((256, 256), F32)],
        compiler_params=pltpu.CompilerParams(vmem_limit_bytes=8 * 2**20 + keys * 1024),
        cost_estimate=pl.CostEstimate(
            flops=4 * rows * width * 1024 * 2, bytes_accessed=keys * 512 + rows * 2048, transcendentals=rows * 2048
        ),
    )(offsets, tiles, queries, key_values, start_cols)


def attend_back(offsets, tiles, queries, key_values, start_rows, inverse, attended, grads):
    rows, width = queries.shape
    keys = key_values.shape[0]
    return pl.pallas_call(
        attend_back_kernel,
        name="attend_back",
        out_shape=(
            jax.ShapeDtypeStruct((rows, width), BF16),
            jax.ShapeDtypeStruct((keys, width), BF16),
        ),
        in_specs=[pl.BlockSpec(memory_space=SMEM)] * 2 + [pl.BlockSpec(memory_space=VMEM)] * 6,
        out_specs=[pl.BlockSpec(memory_space=VMEM)] * 2,
        scratch_shapes=[
            pltpu.VMEM((keys, HEAD_SIZE), F32),
            pltpu.VMEM((keys, HEAD_SIZE), F32),
            pltpu.VMEM((256, HEAD_SIZE), F32),
        ],
        compiler_params=pltpu.CompilerParams(vmem_limit_bytes=8 * 2**20 + keys * 2560),
        cost_estimate=pl.CostEstimate(
            flops=10 * rows * width * 1024 * 2, bytes_accessed=keys * 1024 + rows * 4096, transcendentals=rows * 2048
        ),
    )(offsets, tiles, queries, key_values, start_rows, inverse, attended, grads)


def shape_kernel(raw_ref, cos_ref, sin_ref, gain_ref, q_ref, kv_ref):
    cosine = cos_ref[...]
    sine = sin_ref[...]

    def shaped(first, gain):
        value = raw_ref[:, first : first + HEAD_SIZE]
        mean_square = jnp.mean(value * value, axis=-1, keepdims=True)
        value = value * lax.rsqrt(mean_square + EPSILON) * gain
        return value * cosine + pltpu.roll(value, HEAD_SIZE // 2, 1) * sine

    for head in range(2):
        columns = slice(head * HEAD_SIZE, (head + 1) * HEAD_SIZE)
        q_ref[:, columns] = (shaped(head * HEAD_SIZE, gain_ref[0:1, :]) * HEAD_SIZE**-0.5).astype(BF16)
    kv_ref[:, :HEAD_SIZE] = shaped(2 * HEAD_SIZE, gain_ref[1:2, :]).astype(BF16)
    kv_ref[:, HEAD_SIZE:] = raw_ref[:, 3 * HEAD_SIZE :].astype(BF16)


def shape_back_kernel(raw_ref, grad_ref, cos_ref, sin_ref, gain_ref, low_ref, gain_grad_ref, *, heads, gain_row, factor):
    @pl.when(pl.program_id(0) == 0)
    def _():
        gain_grad_ref[...] = jnp.zeros_like(gain_grad_ref)

    cosine = cos_ref[...]
    sine = sin_ref[...]
    gain = gain_ref[gain_row : gain_row + 1, :]
    total = jnp.zeros((8, HEAD_SIZE), F32)
    for head in range(heads):
        columns = slice(head * HEAD_SIZE, (head + 1) * HEAD_SIZE)
        value = raw_ref[:, columns]
        grad = grad_ref[:, columns].astype(F32) * factor
        grad = grad * cosine - pltpu.roll(grad, HEAD_SIZE // 2, 1) * sine
        rho = lax.rsqrt(jnp.mean(value * value, axis=-1, keepdims=True) + EPSILON)
        unit = value * rho
        total = total + jnp.sum((grad * unit).reshape(-1, 8, HEAD_SIZE), axis=0)
        scaled = grad * gain
        inner = jnp.mean(scaled * unit, axis=-1, keepdims=True)
        low_ref[:, columns] = (rho * (scaled - unit * inner)).astype(BF16)
    if heads == 1:
        low_ref[:, HEAD_SIZE:] = grad_ref[:, HEAD_SIZE:].astype(BF16)
    gain_grad_ref[...] += total


ROW_TILE = 256


def shape_heads(raw, cosine, sine, gains):
    rows = raw.shape[0]
    block = lambda width: pl.BlockSpec((ROW_TILE, width), lambda i: (i, 0))
    return pl.pallas_call(
        shape_kernel,
        name="shape_heads",
        grid=(rows // ROW_TILE,),
        out_shape=(jax.ShapeDtypeStruct((rows, 256), BF16), jax.ShapeDtypeStruct((rows, 256), BF16)),
        in_specs=[block(512), block(128), block(128), pl.BlockSpec((2, 128), lambda i: (0, 0))],
        out_specs=[block(256), block(256)],
        compiler_params=pltpu.CompilerParams(vmem_limit_bytes=8 * 2**20),
        cost_estimate=pl.CostEstimate(flops=rows * 512 * 20, bytes_accessed=rows * 4096, transcendentals=rows * 3),
    )(raw, cosine, sine, gains)


def shape_back(raw, grads, cosine, sine, gains, heads, column, gain_row, factor):
    rows = raw.shape[0]
    block = lambda width, at=0: pl.BlockSpec((ROW_TILE, width), lambda i: (i, at))
    return pl.pallas_call(
        functools.partial(shape_back_kernel, heads=heads, gain_row=gain_row, factor=factor),
        name="shape_back",
        grid=(rows // ROW_TILE,),
        out_shape=(jax.ShapeDtypeStruct((rows, 256), BF16), jax.ShapeDtypeStruct((8, 128), F32)),
        in_specs=[
            block(heads * 128, column),
            block(256),
            block(128),
            block(128),
            pl.BlockSpec((2, 128), lambda i: (0, 0)),
        ],
        out_specs=[block(256), pl.BlockSpec((8, 128), lambda i: (0, 0))],
        compiler_params=pltpu.CompilerParams(vmem_limit_bytes=8 * 2**20),
        cost_estimate=pl.CostEstimate(flops=rows * 256 * 20, bytes_accessed=rows * 4096, transcendentals=rows * 3),
    )(raw, grads, cosine, sine, gains)


def layer(
    sizes,
    tokens,
    out_grad,
    seq_lengths,
    block_deal,
    norm_gain,
    q_weight,
    k_weight,
    v_weight,
    q_gain,
    k_gain,
    o_weight,
    mlp_gain,
    gate_weight,
    up_weight,
    down_weight,
):
    y_count, core_count, zb_count, za_count, x_count = sizes
    pairwise = sizes == (2, 2, 2, 2, 2)
    all_axes = ("y", "core", "zb", "za", "x")
    y_at, core_at, zb_at, za_at, x_at = (lax.axis_index(name) for name in all_axes)
    tok_dev, width = tokens.shape
    blk_rows = q_weight.shape[0]
    group_count = zb_count * x_count
    member_count = y_count * core_count * za_count
    head_count = y_count * core_count
    rows = member_count * tok_dev
    piece = za_count * blk_rows


    def gather_rows(value):
        if not pairwise:
            return lax.all_gather(value, ("y", "core", "za"), axis=0, tiled=True)
        half = tok_dev // 2
        along_y = swap(value, "y")
        along_z = swap(value, "za")
        parts = [value, along_y, along_z, swap(along_z[:half], "y"), swap(along_y[half:], "za")]
        mine = jnp.concatenate(parts, axis=0)
        return jnp.concatenate([mine, swap(mine, "core")], axis=0)

    def scatter_rows(part_of):
        if not pairwise:
            full = part_of(slice(0, rows)).astype(BF16)
            return lax.psum_scatter(full, ("y", "core", "za"), scatter_dimension=0, tiled=True).astype(F32)
        middle = rows // 2
        half = tok_dev // 2
        given = swap(part_of(slice(middle, rows)).astype(BF16), "core")
        kept = part_of(slice(0, middle)) + given.astype(F32)
        own, to_y, to_z, far = (kept[i * tok_dev : (i + 1) * tok_dev] for i in range(4))
        far = far.astype(BF16)
        from_y = swap(far[:half], "y").astype(F32)
        from_z = swap(far[half:], "za").astype(F32)
        z_sum = jnp.concatenate([to_z[:half] + from_y, to_z[half:]], axis=0).astype(BF16)
        y_sum = jnp.concatenate([to_y[:half], to_y[half:] + from_z], axis=0).astype(BF16)
        return own + swap(y_sum, "y").astype(F32) + swap(z_sum, "za").astype(F32)


    def gather_pieces(own, axis):
        if not pairwise:
            return lax.all_gather(own, ("zb", "x"), axis=axis, tiled=True)
        along_z = swap(own, "zb")
        return jnp.concatenate([own, along_z, swap(own, "x"), swap(along_z, "x")], axis=axis)

    def scatter_pieces(part_of, length, axis):
        if not pairwise:
            full = part_of(0, length).astype(BF16)
            return lax.psum_scatter(full, ("zb", "x"), scatter_dimension=axis, tiled=True).astype(F32)
        half, quarter = length // 2, length // 4
        given = swap(part_of(half, length).astype(BF16), "x")
        kept = part_of(0, half) + given.astype(F32)
        given = swap(lax.slice_in_dim(kept, quarter, half, axis=axis).astype(BF16), "zb")
        return lax.slice_in_dim(kept, 0, quarter, axis=axis) + given.astype(F32)

    def in_order(mine, other, axis):
        first = jnp.where(za_at == 0, mine, other)
        second = jnp.where(za_at == 0, other, mine)
        return jnp.concatenate([first, second], axis=axis)

    def gather_weight(part_of, axis):
        mine = part_of(za_at)
        if za_count > 1:
            mine = in_order(mine, swap(part_of(1 - za_at), "za"), axis)
        return gather_pieces(mine, axis)

    def scatter_weight(part_of, axis):
        part = scatter_pieces(part_of, width, axis)
        if za_count == 1:
            return [part]
        first = lax.slice_in_dim(part, 0, blk_rows, axis=axis)
        second = lax.slice_in_dim(part, blk_rows, 2 * blk_rows, axis=axis)
        mine = jnp.where(za_at == 0, first, second)
        other = swap(jnp.where(za_at == 0, second, first).astype(BF16), "za").astype(F32)
        return [jnp.where(za_at == 0, mine, other), jnp.where(za_at == 0, other, mine)]

    def half_of(weight, at, axis):
        size = weight.shape[axis] // za_count
        return lax.dynamic_slice_in_dim(weight, at * size, size, axis=axis)


    def piece_group(index):
        if pairwise:
            return zb_at ^ (index % 2), x_at ^ (index // 2)
        return index // x_count, index % x_count

    def to_pieces(value):
        blocks = []
        for index in range(group_count):
            zb_of, x_of = piece_group(index)
            for za_of in range(za_count):
                block = (zb_of * za_count + za_of) * x_count + x_of
                blocks.append(lax.dynamic_slice_in_dim(value, block * blk_rows, blk_rows, axis=1))
        return jnp.concatenate(blocks, axis=1) if pairwise else value

    def from_pieces(value):
        if not pairwise:
            return value
        blocks = []
        for block in range(group_count * za_count):
            zb_of, za_of, x_of = block // 4, block // 2 % 2, block % 2
            index = (x_at ^ x_of) * 2 + (zb_at ^ zb_of)
            blocks.append(lax.dynamic_slice_in_dim(value, (index * 2 + za_of) * blk_rows, blk_rows, axis=1))
        return jnp.concatenate(blocks, axis=1)


    per_span = head_count // 2
    member = jnp.arange(member_count, dtype=jnp.int32)
    if pairwise:
        member_y, member_za, member_core = y_at ^ (member % 2), za_at ^ (member // 2 % 2), core_at ^ (member // 4)
    else:
        member_za = member % za_count
        member_core = member // za_count % core_count
        member_y = member // (za_count * core_count)
    group = jnp.arange(group_count, dtype=jnp.int32)
    group_zb, group_x = piece_group(group)
    member_head = member_y * core_count + member_core
    span_table = jnp.arange(block_deal.shape[0], dtype=jnp.int32)

    def natural_tile(zb_of, x_of):
        blk = (zb_of * za_count + member_za) * x_count + x_of
        entry = 2 * blk + member_head // per_span
        span = jnp.sum(
            jnp.where(entry[..., None] == span_table, block_deal, 0), axis=-1, dtype=jnp.int32
        )
        return span * per_span + member_head % per_span

    query_tile = natural_tile(zb_at, x_at)
    key_tile = natural_tile(group_zb[:, None], group_x[:, None]).reshape(-1)
    tile_ids = jnp.arange(key_tile.shape[0], dtype=jnp.int32)
    offsets = jnp.sum(
        jnp.where(key_tile[None, :] == tile_ids[:, None], tile_ids[None, :] * tok_dev, 0), axis=1, dtype=jnp.int32
    )
    natural = query_tile[:, None] * tok_dev + jnp.arange(tok_dev, dtype=jnp.int32)[None, :]
    seq_ids = jnp.arange(seq_lengths.shape[0], dtype=jnp.int32)
    seq_ends = jnp.sum(jnp.where(seq_ids[None, :] <= seq_ids[:, None], seq_lengths[None, :], 0), axis=1, dtype=jnp.int32)
    starts = jnp.max(jnp.where(seq_ends <= natural[..., None], seq_ends, 0), axis=-1)
    tiles = jnp.stack([query_tile, starts[:, 0] // (2 * tok_dev), query_tile // 2])
    start_rows = jnp.stack([starts, starts], axis=1)
    start_cols = jnp.broadcast_to(starts.reshape(rows, 1), (rows, 128))
    places = (natural - starts).reshape(rows)
    half_width = HEAD_SIZE // 2
    frequency = jnp.power(ROPE_BASE, -jnp.arange(half_width, dtype=F32) * (2.0 / HEAD_SIZE))
    angles = places.astype(F32)[:, None] * frequency[None, :]
    cosine = jnp.cos(angles)
    sine = jnp.sin(angles)
    cosine = jnp.concatenate([cosine, cosine], axis=1)
    sine = jnp.concatenate([-sine, sine], axis=1)


    q_width = q_weight.shape[1] // za_count
    k_width = k_weight.shape[1] // za_count
    qkv_width = q_width + 2 * k_width
    gain_pad = 16

    gain_row = jnp.concatenate([norm_gain, mlp_gain])
    head_gains = jnp.concatenate([q_gain, k_gain])

    def gain_rows():
        top = jnp.pad(gain_row, (0, qkv_width - gain_row.shape[0]))[None]
        bottom = jnp.pad(head_gains, (0, qkv_width - head_gains.shape[0]))[None]
        return jnp.concatenate([top, bottom, jnp.zeros((gain_pad - 2, qkv_width), BF16)], axis=0)

    def qkv_part(at):
        return jnp.concatenate(
            [half_of(q_weight, at, 1), half_of(k_weight, at, 1), half_of(v_weight, at, 1), ], axis=1
        )

    padded = blk_rows + gain_pad
    own_gain_rows = gain_rows()
    qkv_all = gather_weight(lambda at: jnp.concatenate([qkv_part(at), own_gain_rows], axis=0), 0)
    qkv_all = qkv_all.reshape(group_count * za_count, padded, qkv_width)
    qkv_cols = qkv_all[:, :blk_rows].reshape(width, qkv_width)
    gains = qkv_all[:, blk_rows, : 2 * blk_rows].astype(F32)
    gain_one = gains[:, :blk_rows].reshape(1, width)
    gain_two = gains[:, blk_rows:].reshape(1, width)
    small = q_gain.shape[0]
    head_parts = qkv_all[:, blk_rows + 1, : 2 * small].astype(F32).reshape(group_count * za_count, 2, small)

    def head_gain(which):
        return from_small(head_parts[:, which])

    def from_small(parts):
        if not pairwise:
            return parts.reshape(1, -1)
        rows_of = []
        for block in range(8):
            zb_of, za_of, x_of = block // 4, block // 2 % 2, block % 2
            index = ((x_at ^ x_of) * 2 + (zb_at ^ zb_of)) * 2 + za_of
            rows_of.append(lax.dynamic_slice_in_dim(parts, index, 1, axis=0))
        return jnp.concatenate(rows_of, axis=1)

    qk_gains = jnp.concatenate([head_gain(0), head_gain(1)], axis=0)


    local_low = to_pieces(tokens)
    local_rows = local_low.astype(F32)
    input_rows = gather_rows(local_low).astype(F32)
    o_cols = gather_weight(lambda at: half_of(o_weight, at, 0), 1)
    gu_cols = gather_weight(
        lambda at: jnp.concatenate([half_of(gate_weight, at, 1), half_of(up_weight, at, 1)], axis=1), 0
    )
    down_cols = gather_weight(lambda at: half_of(down_weight, at, 0), 1)
    grad_local = to_pieces(out_grad)
    grad_rows = gather_rows(grad_local)

    def unit_rows(value):
        return value * lax.rsqrt(jnp.mean(value * value, axis=-1, keepdims=True) + EPSILON)

    input_unit = unit_rows(input_rows)
    normed = (input_unit * gain_one).astype(BF16)
    raw = matmul(normed, qkv_cols)
    queries, kv_own = shape_heads(raw, cosine, sine, qk_gains)
    key_values = gather_pieces(kv_own, 0)
    attn_low, inverse = attend(offsets, tiles, queries, key_values, start_cols)
    residual = local_rows + scatter_rows(lambda at: matmul(attn_low[at], o_cols))


    rho_two = lax.rsqrt(jnp.mean(residual * residual, axis=-1, keepdims=True) + EPSILON)
    unit_two = residual * rho_two
    mlp_rows = gather_rows((unit_two * gain_two).astype(BF16))
    ff = gu_cols.shape[1] // 2
    gate_up = matmul(mlp_rows, gu_cols)
    gate_act, up_act = gate_up[:, :ff], gate_up[:, ff:]
    sig = jax.nn.sigmoid(gate_act)
    silu = gate_act * sig
    hidden = (silu * up_act).astype(BF16)
    hidden_grad = contract_cols(grad_rows, down_cols)
    gate_low = (hidden_grad * up_act * (sig * (1.0 + gate_act * (1.0 - sig)))).astype(BF16)
    up_low = (hidden_grad * silu).astype(BF16)
    gu_low = jnp.concatenate([gate_low, up_low], axis=1)
    mlp_in_grad = scatter_rows(lambda at: contract_cols(gu_low[at], gu_cols))

    down_parts = scatter_weight(lambda lo, hi: contract_rows(hidden, grad_rows[:, lo:hi]), 1)
    gate_parts = scatter_weight(lambda lo, hi: contract_rows(mlp_rows[:, lo:hi], gate_low), 0)
    up_parts = scatter_weight(lambda lo, hi: contract_rows(mlp_rows[:, lo:hi], up_low), 0)
    block_out = residual + scatter_rows(lambda at: matmul(hidden[at], down_cols))

    gain_two_part = jnp.sum(mlp_in_grad * unit_two, axis=0, keepdims=True)
    scaled = mlp_in_grad * gain_two
    inner = jnp.mean(scaled * unit_two, axis=-1, keepdims=True)
    residual_grad = grad_local.astype(F32) + rho_two * (scaled - unit_two * inner)


    branch_rows = gather_rows(residual_grad.astype(BF16))
    attn_grad = contract_cols(branch_rows, o_cols).astype(BF16)
    query_grad, kv_grads = attend_back(
        offsets, tiles, queries, key_values, start_rows, inverse, attn_low, attn_grad
    )
    o_parts = scatter_weight(lambda lo, hi: contract_rows(attn_low, branch_rows[:, lo:hi]), 1)
    kv_grad = scatter_pieces(lambda lo, hi: kv_grads[lo:hi].astype(F32), kv_grads.shape[0], 0).astype(BF16)
    q_low, q_gain_part = shape_back(raw, query_grad, cosine, sine, qk_gains, 2, 0, 0, HEAD_SIZE**-0.5)
    kv_low, k_gain_part = shape_back(raw, kv_grad, cosine, sine, qk_gains, 1, 2, 1, 1.0)
    low = jnp.concatenate([q_low, kv_low], axis=1)

    gain_one_parts = []

    def input_terms(at):
        terms = contract_cols(low[at], qkv_cols)
        gain_one_parts.append(jnp.sum(terms * input_unit[at], axis=0, keepdims=True))
        return terms

    input_grad = scatter_rows(input_terms)
    qkv_parts = scatter_weight(lambda lo, hi: contract_rows(normed[:, lo:hi], low), 0)

    gain_sum = jnp.concatenate(
        [
            from_pieces(sum(gain_one_parts)),
            from_pieces(gain_two_part),
            jnp.sum(q_gain_part, axis=0, keepdims=True),
            jnp.sum(k_gain_part, axis=0, keepdims=True),
        ],
        axis=1,
    )
    if pairwise:
        for name in ("core", "y", "za", "x", "zb"):
            gain_sum = gain_sum + swap(gain_sum, name)
    else:
        gain_sum = lax.psum(gain_sum, all_axes)

    unit_one = local_rows * (rho_one := lax.rsqrt(jnp.mean(local_rows * local_rows, axis=-1, keepdims=True) + EPSILON))
    scaled = input_grad * gain_one
    inner = jnp.mean(scaled * unit_one, axis=-1, keepdims=True)
    in_grad = residual_grad + rho_one * (scaled - unit_one * inner)

    device = (((y_at * core_count + core_at) * zb_count + zb_at) * za_count + za_at) * x_count + x_at
    device_count = head_count * zb_count * za_count * x_count

    def own_slice(first, length):
        share = length // device_count
        return lax.dynamic_slice_in_dim(gain_sum[0], first + device * share, share, axis=0)

    def join(parts, lo, hi, axis):
        cut = [lax.slice_in_dim(part, lo, hi, axis=axis) for part in parts]
        return jnp.concatenate(cut, axis=axis)

    return (
        from_pieces(block_out).astype(BF16),
        from_pieces(in_grad),
        own_slice(0, width),
        join(qkv_parts, 0, q_width, 1),
        join(qkv_parts, q_width, q_width + k_width, 1),
        join(qkv_parts, q_width + k_width, qkv_width, 1),
        own_slice(2 * width, HEAD_SIZE),
        own_slice(2 * width + HEAD_SIZE, HEAD_SIZE),
        jnp.concatenate(o_parts, axis=0),
        own_slice(width, width),
        jnp.concatenate(gate_parts, axis=1),
        jnp.concatenate(up_parts, axis=1),
        jnp.concatenate(down_parts, axis=0),
    )


def solution(mesh):
    heads, blks = mesh.shape["head"], mesh.shape["blk"]
    za_count = KEY_VALUE_HEADS // heads
    side = math.isqrt(blks // za_count)
    sizes = (heads // 2, 2, side, za_count, side)
    names = ("y", "core", "zb", "za", "x")
    devices = mesh.devices.reshape(sizes)
    inner = Mesh(devices, names)
    head, blk = ("y", "core"), ("zb", "za", "x")
    rows, in_weight, out_weight, gain = P(names, None), P(blk, head), P(head, blk), P(blk)
    return jax.shard_map(
        functools.partial(layer, sizes),
        mesh=inner,
        in_specs=(
            rows,
            rows,
            P(),
            P(),
            gain,
            in_weight,
            in_weight,
            in_weight,
            gain,
            gain,
            out_weight,
            gain,
            in_weight,
            in_weight,
            out_weight,
        ),
        out_specs=(
            rows,
            rows,
            P(names),
            in_weight,
            in_weight,
            in_weight,
            P(names),
            P(names),
            out_weight,
            P(names),
            in_weight,
            in_weight,
            out_weight,
        ),
        check_vma=False,
    )
```

time: 1770 us -> 807 us (0.46)
  waiting for transfers between devices: 1320 us -> 437 us
  matrix products: 205 us -> 79.8 us
  starting transfers between devices: 6.54 us -> 92.8 us
  blocking collectives: 80.8 us -> 0 us
  local copies, waits for them, and re-layouts: 38 us -> 104 us
  other arithmetic: 89.5 us -> 54 us
  Pallas kernels: 0 us -> 27 us
    reduce_scatter x11 -> x0, waiting for transfers between devices: 643 us -> none  [the longest x1 119 us: shards(): lax.psum_scatter(down_wgrad.astype(jnp.bfloat16), 'blk', scatter_dimensio...]
    all_gather x12 -> x0, waiting for transfers between devices: 517 us -> none  [the longest x1 102 us: shards(): lax.all_gather(down_weight, 'blk', axis=1, tiled=True)]
    ppermute x16 -> x81, waiting for transfers between devices: 156 us -> 437 us  [swap(): return lax.ppermute(value, axis, SWAP)]
    dot_general x63 -> x22, matrix products: 205 us -> 79.8 us  [the longest x6 30 us: contract_cols(): lax.dot_general(left, right, PAIRS_OF_COLS, preferred_element_type=F32)]
    ppermute x16 -> x81, starting transfers between devices: 4.13 us -> 92.8 us  [swap(): return lax.ppermute(value, axis, SWAP)]
    unnamed x125 -> x237, local copies, waits for them, and re-layouts: 13.1 us -> 70.6 us
    convert_element_type x35 -> x9, other arithmetic: 46 us -> 2.57 us  [the longest x1 1.34 us: layer(): scatter_pieces(lambda lo, hi: kv_grads[lo:hi].astype(F32), kv_grads.shape...]
    unnamed x3 -> x0, blocking collectives: 40.8 us -> none
  transfers between devices with their start and end apart: 39 -> 81, of which waited for: 36 -> 39; matrix products, arithmetic and copies ran while one was open for 12% -> 23% of each run, Pallas kernels for 0% -> 2%
where the time goes in v1:
time: 807 us; the launch traced here: 798 us
  waiting for transfers between devices  437 us (54%)
  local copies, waits for them, and re-layouts  104 us (13%)
  starting transfers between devices  92.8 us (11%)
  matrix products  79.8 us (10%)
  other arithmetic  54 us (7%)
  Pallas kernels  27 us (3%)
    ppermute x81, waiting for transfers between devices, swap(): return lax.ppermute(value, axis, SWAP)  437 us
    ppermute x81, starting transfers between devices, swap(): return lax.ppermute(value, axis, SWAP)  92.8 us
    unnamed x237, local copies, waits for them, and re-layouts  70.6 us
    dot_general x6, matrix products, contract_cols(): lax.dot_general(left, right, PAIRS_OF_COLS, preferred_element_type=F32)  30 us
    dot_general x10, matrix products, contract_rows(): lax.dot_general(left, right, PAIRS_OF_ROWS, preferred_element_type=F32)  25.5 us
    dot_general x6, matrix products, matmul(): return jnp.dot(left, right, preferred_element_type=F32)  24.3 us
  transfers between devices with their start and end apart: 81, of which 39 were waited for; matrix products, arithmetic and copies ran while one was open for 23% of the time, Pallas kernels for 2%

profile of v1, /device:TPU:0, one launch (start us, length us, event | category | flops | bytes accessed | tf_op | source)
XLA Modules:
  0.0 797.9 jit_solution(16221295178455733937)
XLA Ops:
  32.8 3.0 fusion.85
  52.6 6.8 collective-permute-done.3
  62.0 4.3 collective-permute-done.6
  70.2 5.8 collective-permute-done.7
  76.0 11.5 %collective-permute-done.8 = bf16[544,512]{1,0:T(8,128)(2,1)S(1)} collective-permute-done((bf16[544,512]{1,0:T(8,128)(2,1)S(1)}, bf16[544,512]{1,0:T(8,128)(2,1)S(1)}, u32[]{:S(2)}, u32[]{:S(2)}) %collective-permute-start.8) | collective-permute-done | bytes 557088 | tf_op jit(solution)/shard_map/ppermute | solution.py:38
  89.5 3.1 constant_dynamic-update-slice_fusion.20
  92.6 3.1 fusion
  95.7 6.8 convert_multiply_fusion
  111.7 32.1 %collective-permute-done.13 = bf16[256,512]{1,0:T(8,128)(2,1)S(1)} collective-permute-done((bf16[256,512]{1,0:T(8,128)(2,1)S(1)}, bf16[256,512]{1,0:T(8,128)(2,1)S(1)}, u32[]{:S(2)}, u32[]{:S(2)}) %collective-permute-start.13) | collective-permute-done | bytes 262176 | tf_op jit(solution)/shard_map/ppermute | solution.py:38
  148.9 4.1 collective-permute-done.15
  153.9 10.4 %collective-permute-done.10 = bf16[1024,256]{1,0:T(8,128)(2,1)S(1)} collective-permute-done((bf16[1024,256]{1,0:T(8,128)(2,1)S(1)}, bf16[1024,256]{1,0:T(8,128)(2,1)S(1)}, u32[]{:S(2)}, u32[]{:S(2)}) %collective-permute-start.10) | collective-permute-done | bytes 524320 | tf_op jit(solution)/shard_map/ppermute | solution.py:38
  164.3 9.0 %collective-permute-done.11 = bf16[1024,256]{1,0:T(8,128)(2,1)S(1)} collective-permute-done((bf16[1024,256]{1,0:T(8,128)(2,1)S(1)}, bf16[1024,256]{1,0:T(8,128)(2,1)S(1)}, u32[]{:S(2)}, u32[]{:S(2)}) %collective-permute-start.11) | collective-permute-done | bytes 524320 | tf_op jit(solution)/shard_map/ppermute | solution.py:38
  173.6 9.2 %attend.1 = (bf16[1024,256]{1,0:T(8,128)(2,1)S(1)}, f32[8,2,128]{2,1,0:T(2,128)S(1)}) custom-call(s32[32]{0:T(128)S(1)} %select_reduce_fusion.1.off_ref, s32[3,8]{1,0:T(4,128)S(1)} %pad_add_fusion.1.tile_ref, bf16[1024,256]{1,0:T(8,128)(2,1)S(1)} %get-tuple-element.23.q_ref, bf16[4096,256]{1,0:T(8,128)(2,1)S(1)} %constant_dynamic-update-slice_fusion.38.kv_ref, ...), custom_call_target="tpu_custom_call" | custom-call | flops 2147483648 | bytes 4194304 | tf_op jit(solution)/shard_map/attend/pallas_call | solution.py:155
  191.2 22.4 %collective-permute-done.30 = bf16[768,256]{1,0:T(8,128)(2,1)S(1)} collective-permute-done((bf16[768,256]{1,0:T(8,128)(2,1)S(1)}, bf16[768,256]{1,0:T(8,128)(2,1)S(1)}, u32[]{:S(2)}, u32[]{:S(2)}) %collective-permute-start.30) | collective-permute-done | bytes 393248 | tf_op jit(solution)/shard_map/ppermute | solution.py:38
  215.4 4.2 collective-permute-start.31
  231.3 16.5 %collective-permute-done.17 = bf16[64,2048]{1,0:T(8,128)(2,1)S(1)} collective-permute-done((bf16[64,2048]{1,0:T(8,128)(2,1)S(1)}, bf16[64,2048]{1,0:T(8,128)(2,1)S(1)}, u32[]{:S(2)}, u32[]{:S(2)}) %collective-permute-start.17) | collective-permute-done | bytes 262176 | tf_op jit(solution)/shard_map/ppermute | solution.py:38
  253.3 7.6 collective-permute-done.18
  260.9 4.4 collective-permute-done.20
  269.0 4.1 collective-permute-start.27
  277.5 13.6 %collective-permute-done.22 = bf16[128,2048]{1,0:T(8,128)(2,1)S(1)} collective-permute-done((bf16[128,2048]{1,0:T(8,128)(2,1)S(1)}, bf16[128,2048]{1,0:T(8,128)(2,1)S(1)}, u32[]{:S(2)}, u32[]{:S(2)}) %collective-permute-start.22) | collective-permute-done | bytes 524320 | tf_op jit(solution)/shard_map/ppermute | solution.py:38
  300.4 18.3 %collective-permute-done.24 = bf16[64,2048]{1,0:T(8,128)(2,1)S(1)} collective-permute-done((bf16[64,2048]{1,0:T(8,128)(2,1)S(1)}, bf16[64,2048]{1,0:T(8,128)(2,1)S(1)}, u32[]{:S(2)}, u32[]{:S(2)}) %collective-permute-start.24) | collective-permute-done | bytes 262176 | tf_op jit(solution)/shard_map/ppermute | solution.py:38
  323.6 17.9 %collective-permute-done.27 = bf16[512,1536]{1,0:T(8,128)(2,1)} collective-permute-done((bf16[512,1536]{1,0:T(8,128)(2,1)}, bf16[512,1536]{1,0:T(8,128)(2,1)}, u32[]{:S(2)}, u32[]{:S(2)}) %collective-permute-start.27) | collective-permute-done | bytes 1572896 | tf_op jit(solution)/shard_map/ppermute | solution.py:38
  357.8 23.8 %collective-permute-done.29 = bf16[512,1536]{1,0:T(8,128)(2,1)} collective-permute-done((bf16[512,1536]{1,0:T(8,128)(2,1)}, bf16[512,1536]{1,0:T(8,128)(2,1)}, u32[]{:S(2)}, u32[]{:S(2)}) %collective-permute-start.29) | collective-permute-done | bytes 1572896 | tf_op jit(solution)/shard_map/ppermute | solution.py:38
  386.1 9.2 %fusion.143 = f32[1024,1536]{1,0:T(8,128)S(1)} fusion(bf16[1024,2048]{1,0:T(8,128)(2,1)S(1)} %constant_dynamic-update-slice_fusion.52, bf16[2048,1536]{1,0:T(8,128)(2,1)} %constant_dynamic-update-slice_fusion.58), kind=kOutput, calls=%fused_computation.493 | convolution fusion | flops 6442450944 | bytes 16777216 | tf_op jit(solution)/shard_map/dot_general | solution.py:26
  395.3 6.3 multiply_convert_fusion.2
  412.7 5.0 convolution_convert_fusion.2
  419.4 6.3 convolution_convert_fusion.1
  426.3 16.0 %collective-permute-done.78 = bf16[768,1024]{1,0:T(8,128)(2,1)} collective-permute-done((bf16[768,1024]{1,0:T(8,128)(2,1)}, bf16[768,1024]{1,0:T(8,128)(2,1)}, u32[]{:S(2)}, u32[]{:S(2)}) %collective-permute-start.78) | collective-permute-done | bytes 1572896 | tf_op jit(solution)/shard_map/ppermute | solution.py:38
  442.3 3.2 convert_add_fusion.4
  445.7 30.1 %collective-permute-done.75 = bf16[1024,768]{0,1:T(8,128)(2,1)S(1)} collective-permute-done((bf16[1024,768]{0,1:T(8,128)(2,1)}, bf16[1024,768]{0,1:T(8,128)(2,1)S(1)}, u32[]{:S(2)}, u32[]{:S(2)}) %collective-permute-start.75) | collective-permute-done | bytes 1572896 | tf_op jit(solution)/shard_map/ppermute | solution.py:38
  477.9 30.4 %collective-permute-done.72 = bf16[1024,768]{0,1:T(8,128)(2,1)S(1)} collective-permute-done((bf16[1024,768]{0,1:T(8,128)(2,1)}, bf16[1024,768]{0,1:T(8,128)(2,1)S(1)}, u32[]{:S(2)}, u32[]{:S(2)}) %collective-permute-start.72) | collective-permute-done | bytes 1572896 | tf_op jit(solution)/shard_map/ppermute | solution.py:38
  510.3 3.7 fusion.141
  515.4 8.7 %fusion.140 = (bf16[512,2048]{1,0:T(8,128)(2,1)}, f32[512,2048]{1,0:T(8,128)S(1)}) fusion(bf16[512,2048]{1,0:T(8,128)(2,1)} %collective-permute-done.44, bf16[2048,1536]{1,0:T(8,128)(2,1)} %constant_dynamic-update-slice_fusion.58, bf16[1024,768]{1,0:T(8,128)(2,1)} %copy-done.63, bf16[1024,768]{1,0:T(8,128)(2,1)} %copy-done.65), kind=kOutput, calls=%fused_computation.490 | convolution fusion | flops 3227516928 | bytes 17825792 | tf_op jit(solution)/shard_map/dot_general | solution.py:34
  540.1 16.2 %collective-permute-done.46 = bf16[128,2048]{1,0:T(8,128)(2,1)S(1)} collective-permute-done((bf16[128,2048]{1,0:T(8,128)(2,1)S(1)}, bf16[128,2048]{1,0:T(8,128)(2,1)S(1)}, u32[]{:S(2)}, u32[]{:S(2)}) %collective-permute-start.46) | collective-permute-done | bytes 524320 | tf_op jit(solution)/shard_map/ppermute | solution.py:38
  563.7 27.3 %collective-permute-done.73 = bf16[512,768]{0,1:T(8,128)(2,1)S(1)} collective-permute-done((bf16[512,768]{0,1:T(8,128)(2,1)S(1)}, bf16[512,768]{0,1:T(8,128)(2,1)S(1)}, u32[]{:S(2)}, u32[]{:S(2)}) %collective-permute-start.73) | collective-permute-done | bytes 786464 | tf_op jit(solution)/shard_map/ppermute | solution.py:38
  600.5 7.5 collective-permute-done.52
  629.5 3.5 convolution_convert_fusion.3.grad_ref
  633.2 13.0 %attend_back.1 = (bf16[1024,256]{1,0:T(8,128)(2,1)S(1)}, bf16[4096,256]{1,0:T(8,128)(2,1)S(1)}) custom-call(s32[32]{0:T(128)S(1)} %select_reduce_fusion.1.off_ref, s32[3,8]{1,0:T(4,128)S(1)} %pad_add_fusion.1.tile_ref, bf16[1024,256]{1,0:T(8,128)(2,1)S(1)} %copy-done.6, bf16[4096,256]{1,0:T(8,128)(2,1)S(1)} %copy-done.4, ...), custom_call_target="tpu_custom_call" | custom-call | flops 5368709120 | bytes 8388608 | tf_op jit(solution)/shard_map/attend_back/pallas_call | solution.py:175
  646.2 4.6 collective-permute-start.54
  652.6 22.3 %collective-permute-done.54 = bf16[2048,256]{1,0:T(8,128)(2,1)S(1)} collective-permute-done((bf16[2048,256]{1,0:T(8,128)(2,1)S(1)}, bf16[2048,256]{1,0:T(8,128)(2,1)S(1)}, u32[]{:S(2)}, u32[]{:S(2)}) %collective-permute-start.54) | collective-permute-done | bytes 1048608 | tf_op jit(solution)/shard_map/ppermute | solution.py:38
  689.6 16.0 %collective-permute-done.55 = bf16[1024,256]{1,0:T(8,128)(2,1)} collective-permute-done((bf16[1024,256]{1,0:T(8,128)(2,1)}, bf16[1024,256]{1,0:T(8,128)(2,1)}, u32[]{:S(2)}, u32[]{:S(2)}) %collective-permute-start.55) | collective-permute-done | bytes 524320 | tf_op jit(solution)/shard_map/ppermute | solution.py:38
  713.3 4.0 fusion.1
  728.0 7.9 collective-permute-done.66
  735.9 3.1 convert_add_fusion.7
  743.2 19.5 %collective-permute-done.65 = f32[1,4352]{1,0:T(1,128)S(1)} collective-permute-done((f32[1,4352]{1,0:T(1,128)S(1)}, f32[1,4352]{1,0:T(1,128)S(1)}, u32[]{:S(2)}, u32[]{:S(2)}) %collective-permute-start.65) | collective-permute-done | bytes 17440 | tf_op jit(solution)/shard_map/ppermute | solution.py:38
  769.3 4.0 collective-permute-done.68
  774.2 3.8 collective-permute-done.57
  784.6 7.6 collective-permute-done.58
  (543 shorter events, 273.7 us)
Async XLA Ops:
  13.9 31.8 %collective-permute-start = (bf16[128,2048]{1,0:T(8,128)(2,1)S(1)}, bf16[128,2048]{1,0:T(8,128)(2,1)}, u32[]{:S(2)}, u32[]{:S(2)}) collective-permute-start(bf16[128,2048]{1,0:T(8,128)(2,1)S(1)} %get-tuple-element.201), channel_id=1, source_target_pairs={{0,16},{16,0},{1,17},{17,1},{2,18},{18,2},{3,19},{19,3},{4,20},{20... | collective-permute-start | bytes 1572872 | tf_op jit(solution)/shard_map/ppermute | solution.py:38
  16.9 26.3 %collective-permute-start.1 = (bf16[128,2048]{1,0:T(8,128)(2,1)S(1)}, bf16[128,2048]{1,0:T(8,128)(2,1)}, u32[]{:S(2)}, u32[]{:S(2)}) collective-permute-start(bf16[128,2048]{1,0:T(8,128)(2,1)S(1)} %get-tuple-element.201), channel_id=1, source_target_pairs={{0,2},{2,0},{1,3},{3,1},{4,6},{6,4},{5,7},{7,5},{8,10},{10,8},{9,1... | collective-permute-start | bytes 1572872 | tf_op jit(solution)/shard_map/ppermute | solution.py:38
  24.5 196.8 %collective-permute-start.39 = (bf16[128,2048]{1,0:T(8,128)(2,1)}, bf16[128,2048]{1,0:T(8,128)(2,1)}, u32[]{:S(2)}, u32[]{:S(2)}) collective-permute-start(bf16[128,2048]{1,0:T(8,128)(2,1)} %get-tuple-element.178), channel_id=1, source_target_pairs={{0,16},{16,0},{1,17},{17,1},{2,18},{18,2},{3,19},{19,3},{4,20},{20... | collective-permute-start | bytes 1572872 | tf_op jit(solution)/shard_map/ppermute | solution.py:38
  26.2 41.6 %collective-permute-start.12 = (bf16[256,256]{1,0:T(8,128)(2,1)}, bf16[256,256]{1,0:T(8,128)(2,1)}, u32[]{:S(2)}, u32[]{:S(2)}) collective-permute-start(bf16[256,256]{1,0:T(8,128)(2,1)} %constant_dynamic-slice_fusion.9), channel_id=1, source_target_pairs={{0,2},{2,0},{1,3},{3,1},{4,6},{6,4},{5,7},{7,5},{8,10},{10,8},{9,1... | collective-permute-start | bytes 393224 | tf_op jit(solution)/shard_map/ppermute | solution.py:38
  40.6 25.7 %collective-permute-start.6 = (bf16[544,512]{1,0:T(8,128)(2,1)S(1)}, bf16[544,512]{1,0:T(8,128)(2,1)S(1)}, u32[]{:S(2)}, u32[]{:S(2)}) collective-permute-start(bf16[544,512]{1,0:T(8,128)(2,1)S(1)} %pad_maximum_fusion.9), channel_id=1, source_target_pairs={{0,4},{4,0},{1,5},{5,1},{2,6},{6,2},{3,7},{7,3},{8,12},{12,8},{9,1... | collective-permute-start | bytes 1671176 | tf_op jit(solution)/shard_map/ppermute | solution.py:38
  60.2 29.2 %collective-permute-start.4 = (bf16[512,2048]{1,0:T(8,128)(2,1)}, bf16[512,2048]{1,0:T(8,128)(2,1)}, u32[]{:S(2)}, u32[]{:S(2)}) collective-permute-start(bf16[512,2048]{1,0:T(8,128)(2,1)} %get-tuple-element.215), channel_id=1, source_target_pairs={{0,8},{8,0},{1,9},{9,1},{2,10},{10,2},{3,11},{11,3},{4,12},{12,4},... | collective-permute-start | bytes 6291464 | tf_op jit(solution)/shard_map/ppermute | solution.py:38
  66.3 21.2 %collective-permute-start.8 = (bf16[544,512]{1,0:T(8,128)(2,1)S(1)}, bf16[544,512]{1,0:T(8,128)(2,1)S(1)}, u32[]{:S(2)}, u32[]{:S(2)}) collective-permute-start(bf16[544,512]{1,0:T(8,128)(2,1)S(1)} %collective-permute-done.6), channel_id=1, source_target_pairs={{0,1},{1,0},{2,3},{3,2},{4,5},{5,4},{6,7},{7,6},{8,9},{9,8},{10,11... | collective-permute-start | bytes 1671176 | tf_op jit(solution)/shard_map/ppermute | solution.py:38
  106.8 39.8 %collective-permute-start.9 = (bf16[1024,256]{1,0:T(8,128)(2,1)S(1)}, bf16[1024,256]{1,0:T(8,128)(2,1)S(1)}, u32[]{:S(2)}, u32[]{:S(2)}) collective-permute-start(bf16[1024,256]{1,0:T(8,128)(2,1)S(1)} %get-tuple-element.24), channel_id=1, source_target_pairs={{0,4},{4,0},{1,5},{5,1},{2,6},{6,2},{3,7},{7,3},{8,12},{12,8},{9,1... | collective-permute-start | bytes 1572872 | tf_op jit(solution)/shard_map/ppermute | solution.py:38
  108.1 35.7 %collective-permute-start.13 = (bf16[256,512]{1,0:T(8,128)(2,1)S(1)}, bf16[256,512]{1,0:T(8,128)(2,1)S(1)}, u32[]{:S(2)}, u32[]{:S(2)}) collective-permute-start(bf16[256,512]{1,0:T(8,128)(2,1)S(1)} %pad_maximum_fusion.26), channel_id=1, source_target_pairs={{0,4},{4,0},{1,5},{5,1},{2,6},{6,2},{3,7},{7,3},{8,12},{12,8},{9,1... | collective-permute-start | bytes 786440 | tf_op jit(solution)/shard_map/ppermute | solution.py:38
  110.0 36.6 %collective-permute-start.14 = (bf16[256,512]{1,0:T(8,128)(2,1)S(1)}, bf16[256,512]{1,0:T(8,128)(2,1)S(1)}, u32[]{:S(2)}, u32[]{:S(2)}) collective-permute-start(bf16[256,512]{1,0:T(8,128)(2,1)S(1)} %pad_maximum_fusion.26), channel_id=1, source_target_pairs={{0,1},{1,0},{2,3},{3,2},{4,5},{5,4},{6,7},{7,6},{8,9},{9,8},{10,11... | collective-permute-start | bytes 786440 | tf_op jit(solution)/shard_map/ppermute | solution.py:38
  146.6 73.0 %collective-permute-start.40 = (bf16[128,2048]{1,0:T(8,128)(2,1)}, bf16[128,2048]{1,0:T(8,128)(2,1)S(1)}, u32[]{:S(2)}, u32[]{:S(2)}) collective-permute-start(bf16[128,2048]{1,0:T(8,128)(2,1)} %get-tuple-element.178), channel_id=1, source_target_pairs={{0,2},{2,0},{1,3},{3,1},{4,6},{6,4},{5,7},{7,5},{8,10},{10,8},{9,1... | collective-permute-start | bytes 1572872 | tf_op jit(solution)/shard_map/ppermute | solution.py:38
  146.7 26.7 %collective-permute-start.11 = (bf16[1024,256]{1,0:T(8,128)(2,1)S(1)}, bf16[1024,256]{1,0:T(8,128)(2,1)S(1)}, u32[]{:S(2)}, u32[]{:S(2)}) collective-permute-start(bf16[1024,256]{1,0:T(8,128)(2,1)S(1)} %collective-permute-done.9), channel_id=1, source_target_pairs={{0,1},{1,0},{2,3},{3,2},{4,5},{5,4},{6,7},{7,6},{8,9},{9,8},{10,11... | collective-permute-start | bytes 1572872 | tf_op jit(solution)/shard_map/ppermute | solution.py:38
  185.0 42.3 %collective-permute-start.16 = (bf16[512,2048]{1,0:T(8,128)(2,1)S(1)}, bf16[512,2048]{1,0:T(8,128)(2,1)S(1)}, u32[]{:S(2)}, u32[]{:S(2)}) collective-permute-start(bf16[512,2048]{1,0:T(8,128)(2,1)S(1)} %convolution_convert_fusion), channel_id=1, source_target_pairs={{0,8},{8,0},{1,9},{9,1},{2,10},{10,2},{3,11},{11,3},{4,12},{12,4},... | collective-permute-start | bytes 6291464 | tf_op jit(solution)/shard_map/ppermute | solution.py:38
  185.1 44.6 %collective-permute-start.26 = (bf16[256,1536]{1,0:T(8,128)(2,1)S(1)}, bf16[256,1536]{1,0:T(8,128)(2,1)S(1)}, u32[]{:S(2)}, u32[]{:S(2)}) collective-permute-start(bf16[256,1536]{1,0:T(8,128)(2,1)S(1)} %pad_maximum_fusion.7), channel_id=1, source_target_pairs={{0,2},{2,0},{1,3},{3,1},{4,6},{6,4},{5,7},{7,5},{8,10},{10,8},{9,1... | collective-permute-start | bytes 2359304 | tf_op jit(solution)/shard_map/ppermute | solution.py:38
  185.7 27.9 %collective-permute-start.30 = (bf16[768,256]{1,0:T(8,128)(2,1)S(1)}, bf16[768,256]{1,0:T(8,128)(2,1)S(1)}, u32[]{:S(2)}, u32[]{:S(2)}) collective-permute-start(bf16[768,256]{1,0:T(8,128)(2,1)S(1)} %constant_dynamic-slice_fusion.4), channel_id=1, source_target_pairs={{0,2},{2,0},{1,3},{3,1},{4,6},{6,4},{5,7},{7,5},{8,10},{10,8},{9,1... | collective-permute-start | bytes 1179656 | tf_op jit(solution)/shard_map/ppermute | solution.py:38
  215.4 78.5 %collective-permute-start.31 = (bf16[768,512]{1,0:T(8,128)(2,1)S(1)}, bf16[768,512]{1,0:T(8,128)(2,1)}, u32[]{:S(2)}, u32[]{:S(2)}) collective-permute-start(bf16[768,512]{1,0:T(8,128)(2,1)S(1)} %pad_maximum_fusion.8), channel_id=1, source_target_pairs={{0,4},{4,0},{1,5},{5,1},{2,6},{6,2},{3,7},{7,3},{8,12},{12,8},{9,1... | collective-permute-start | bytes 2359304 | tf_op jit(solution)/shard_map/ppermute | solution.py:38
  219.7 53.4 %collective-permute-start.41 = (bf16[64,2048]{1,0:T(8,128)(2,1)S(1)}, bf16[64,2048]{1,0:T(8,128)(2,1)S(1)}, u32[]{:S(2)}, u32[]{:S(2)}) collective-permute-start(bf16[64,2048]{1,0:T(8,128)(2,1)S(1)} %slice.461), channel_id=1, source_target_pairs={{0,16},{16,0},{1,17},{17,1},{2,18},{18,2},{3,19},{19,3},{4,20},{20... | collective-permute-start | bytes 786440 | tf_op jit(solution)/shard_map/ppermute | solution.py:38
  222.3 53.2 %collective-permute-start.42 = (bf16[64,2048]{1,0:T(8,128)(2,1)S(1)}, bf16[64,2048]{1,0:T(8,128)(2,1)S(1)}, u32[]{:S(2)}, u32[]{:S(2)}) collective-permute-start(bf16[64,2048]{1,0:T(8,128)(2,1)S(1)} %slice.462), channel_id=1, source_target_pairs={{0,2},{2,0},{1,3},{3,1},{4,6},{6,4},{5,7},{7,5},{8,10},{10,8},{9,1... | collective-permute-start | bytes 786440 | tf_op jit(solution)/shard_map/ppermute | solution.py:38
  267.7 23.4 %collective-permute-start.22 = (bf16[128,2048]{1,0:T(8,128)(2,1)S(1)}, bf16[128,2048]{1,0:T(8,128)(2,1)S(1)}, u32[]{:S(2)}, u32[]{:S(2)}) collective-permute-start(bf16[128,2048]{1,0:T(8,128)(2,1)S(1)} %get-tuple-element.86), channel_id=1, source_target_pairs={{0,2},{2,0},{1,3},{3,1},{4,6},{6,4},{5,7},{7,5},{8,10},{10,8},{9,1... | collective-permute-start | bytes 1572872 | tf_op jit(solution)/shard_map/ppermute | solution.py:38
  269.0 72.5 %collective-permute-start.27 = (bf16[512,1536]{1,0:T(8,128)(2,1)}, bf16[512,1536]{1,0:T(8,128)(2,1)}, u32[]{:S(2)}, u32[]{:S(2)}) collective-permute-start(bf16[512,1536]{1,0:T(8,128)(2,1)} %pad_maximum_fusion.2), channel_id=1, source_target_pairs={{0,4},{4,0},{1,5},{5,1},{2,6},{6,2},{3,7},{7,3},{8,12},{12,8},{9,1... | collective-permute-start | bytes 4718600 | tf_op jit(solution)/shard_map/ppermute | solution.py:38
  275.5 45.8 %collective-permute-start.32 = (bf16[768,512]{1,0:T(8,128)(2,1)S(1)}, bf16[768,512]{1,0:T(8,128)(2,1)S(1)}, u32[]{:S(2)}, u32[]{:S(2)}) collective-permute-start(bf16[768,512]{1,0:T(8,128)(2,1)S(1)} %pad_maximum_fusion.8), channel_id=1, source_target_pairs={{0,1},{1,0},{2,3},{3,2},{4,5},{5,4},{6,7},{7,6},{8,9},{9,8},{10,11... | collective-permute-start | bytes 2359304 | tf_op jit(solution)/shard_map/ppermute | solution.py:38
  292.8 63.1 %collective-permute-start.43 = (bf16[512,2048]{1,0:T(8,128)(2,1)}, bf16[512,2048]{1,0:T(8,128)(2,1)}, u32[]{:S(2)}, u32[]{:S(2)}) collective-permute-start(bf16[512,2048]{1,0:T(8,128)(2,1)} %get-tuple-element.207), channel_id=1, source_target_pairs={{0,8},{8,0},{1,9},{9,1},{2,10},{10,2},{3,11},{11,3},{4,12},{12,4},... | collective-permute-start | bytes 6291464 | tf_op jit(solution)/shard_map/ppermute | solution.py:38
  293.9 59.4 %collective-permute-start.28 = (bf16[512,1536]{1,0:T(8,128)(2,1)}, bf16[512,1536]{1,0:T(8,128)(2,1)}, u32[]{:S(2)}, u32[]{:S(2)}) collective-permute-start(bf16[512,1536]{1,0:T(8,128)(2,1)} %pad_maximum_fusion.2), channel_id=1, source_target_pairs={{0,1},{1,0},{2,3},{3,2},{4,5},{5,4},{6,7},{7,6},{8,9},{9,8},{10,11... | collective-permute-start | bytes 4718600 | tf_op jit(solution)/shard_map/ppermute | solution.py:38
  318.8 29.5 %collective-permute-start.33 = (bf16[768,512]{1,0:T(8,128)(2,1)}, bf16[768,512]{1,0:T(8,128)(2,1)}, u32[]{:S(2)}, u32[]{:S(2)}) collective-permute-start(bf16[768,512]{1,0:T(8,128)(2,1)} %collective-permute-done.31), channel_id=1, source_target_pairs={{0,1},{1,0},{2,3},{3,2},{4,5},{5,4},{6,7},{7,6},{8,9},{9,8},{10,11... | collective-permute-start | bytes 2359304 | tf_op jit(solution)/shard_map/ppermute | solution.py:38
  323.6 60.7 %collective-permute-start.25 = (bf16[512,2048]{1,0:T(8,128)(2,1)}, bf16[512,2048]{1,0:T(8,128)(2,1)}, u32[]{:S(2)}, u32[]{:S(2)}) collective-permute-start(bf16[512,2048]{1,0:T(8,128)(2,1)} %get-tuple-element.211), channel_id=1, source_target_pairs={{0,8},{8,0},{1,9},{9,1},{2,10},{10,2},{3,11},{11,3},{4,12},{12,4},... | collective-permute-start | bytes 6291464 | tf_op jit(solution)/shard_map/ppermute | solution.py:38
  341.4 40.2 %collective-permute-start.29 = (bf16[512,1536]{1,0:T(8,128)(2,1)}, bf16[512,1536]{1,0:T(8,128)(2,1)}, u32[]{:S(2)}, u32[]{:S(2)}) collective-permute-start(bf16[512,1536]{1,0:T(8,128)(2,1)} %collective-permute-done.27), channel_id=1, source_target_pairs={{0,1},{1,0},{2,3},{3,2},{4,5},{5,4},{6,7},{7,6},{8,9},{9,8},{10,11... | collective-permute-start | bytes 4718600 | tf_op jit(solution)/shard_map/ppermute | solution.py:38
  404.6 37.6 %collective-permute-start.78 = (bf16[768,1024]{1,0:T(8,128)(2,1)}, bf16[768,1024]{1,0:T(8,128)(2,1)}, u32[]{:S(2)}, u32[]{:S(2)}) collective-permute-start(bf16[768,1024]{1,0:T(8,128)(2,1)} %fusion.36), channel_id=1, source_target_pairs={{0,1},{1,0},{2,3},{3,2},{4,5},{5,4},{6,7},{7,6},{8,9},{9,8},{10,11... | collective-permute-start | bytes 4718600 | tf_op jit(solution)/shard_map/ppermute | solution.py:38
  409.4 66.4 %collective-permute-start.75 = (bf16[1024,768]{0,1:T(8,128)(2,1)}, bf16[1024,768]{0,1:T(8,128)(2,1)S(1)}, u32[]{:S(2)}, u32[]{:S(2)}) collective-permute-start(bf16[1024,768]{0,1:T(8,128)(2,1)} %fusion.33), channel_id=1, source_target_pairs={{0,1},{1,0},{2,3},{3,2},{4,5},{5,4},{6,7},{7,6},{8,9},{9,8},{10,11... | collective-permute-start | bytes 4718600 | tf_op jit(solution)/shard_map/ppermute | solution.py:38
  417.7 90.6 %collective-permute-start.72 = (bf16[1024,768]{0,1:T(8,128)(2,1)}, bf16[1024,768]{0,1:T(8,128)(2,1)S(1)}, u32[]{:S(2)}, u32[]{:S(2)}) collective-permute-start(bf16[1024,768]{0,1:T(8,128)(2,1)} %fusion.30), channel_id=1, source_target_pairs={{0,1},{1,0},{2,3},{3,2},{4,5},{5,4},{6,7},{7,6},{8,9},{9,8},{10,11... | collective-permute-start | bytes 4718600 | tf_op jit(solution)/shard_map/ppermute | solution.py:38
  419.4 90.9 %collective-permute-start.34 = (bf16[512,2048]{1,0:T(8,128)(2,1)}, bf16[512,2048]{1,0:T(8,128)(2,1)S(1)}, u32[]{:S(2)}, u32[]{:S(2)}) collective-permute-start(bf16[512,2048]{1,0:T(8,128)(2,1)} %convolution_convert_fusion.2), channel_id=1, source_target_pairs={{0,8},{8,0},{1,9},{9,1},{2,10},{10,2},{3,11},{11,3},{4,12},{12,4},... | collective-permute-start | bytes 6291464 | tf_op jit(solution)/shard_map/ppermute | solution.py:38
  425.7 89.7 %collective-permute-start.44 = (bf16[512,2048]{1,0:T(8,128)(2,1)}, bf16[512,2048]{1,0:T(8,128)(2,1)}, u32[]{:S(2)}, u32[]{:S(2)}) collective-permute-start(bf16[512,2048]{1,0:T(8,128)(2,1)} %convolution_convert_fusion.1), channel_id=1, source_target_pairs={{0,8},{8,0},{1,9},{9,1},{2,10},{10,2},{3,11},{11,3},{4,12},{12,4},... | collective-permute-start | bytes 6291464 | tf_op jit(solution)/shard_map/ppermute | solution.py:38
  445.6 165.1 %collective-permute-start.79 = (bf16[768,512]{1,0:T(8,128)(2,1)S(1)}, bf16[768,512]{1,0:T(8,128)(2,1)}, u32[]{:S(2)}, u32[]{:S(2)}) collective-permute-start(bf16[768,512]{1,0:T(8,128)(2,1)S(1)} %slice.729), channel_id=1, source_target_pairs={{0,4},{4,0},{1,5},{5,1},{2,6},{6,2},{3,7},{7,3},{8,12},{12,8},{9,1... | collective-permute-start | bytes 2359304 | tf_op jit(solution)/shard_map/ppermute | solution.py:38
  477.9 60.6 %collective-permute-start.76 = (bf16[512,768]{0,1:T(8,128)(2,1)S(1)}, bf16[512,768]{0,1:T(8,128)(2,1)}, u32[]{:S(2)}, u32[]{:S(2)}) collective-permute-start(bf16[512,768]{0,1:T(8,128)(2,1)S(1)} %slice.730), channel_id=1, source_target_pairs={{0,4},{4,0},{1,5},{5,1},{2,6},{6,2},{3,7},{7,3},{8,12},{12,8},{9,1... | collective-permute-start | bytes 2359304 | tf_op jit(solution)/shard_map/ppermute | solution.py:38
  530.7 28.1 %collective-permute-start.36 = (bf16[128,2048]{1,0:T(8,128)(2,1)S(1)}, bf16[128,2048]{1,0:T(8,128)(2,1)S(1)}, u32[]{:S(2)}, u32[]{:S(2)}) collective-permute-start(bf16[128,2048]{1,0:T(8,128)(2,1)S(1)} %pad_maximum_fusion.14), channel_id=1, source_target_pairs={{0,16},{16,0},{1,17},{17,1},{2,18},{18,2},{3,19},{19,3},{4,20},{20... | collective-permute-start | bytes 1572872 | tf_op jit(solution)/shard_map/ppermute | solution.py:38
  532.4 26.5 %collective-permute-start.38 = (bf16[128,2048]{1,0:T(8,128)(2,1)S(1)}, bf16[128,2048]{1,0:T(8,128)(2,1)S(1)}, u32[]{:S(2)}, u32[]{:S(2)}) collective-permute-start(bf16[128,2048]{1,0:T(8,128)(2,1)S(1)} %pad_maximum_fusion.15), channel_id=1, source_target_pairs={{0,2},{2,0},{1,3},{3,1},{4,6},{6,4},{5,7},{7,5},{8,10},{10,8},{9,1... | collective-permute-start | bytes 1572872 | tf_op jit(solution)/shard_map/ppermute | solution.py:38
  556.3 34.7 %collective-permute-start.73 = (bf16[512,768]{0,1:T(8,128)(2,1)S(1)}, bf16[512,768]{0,1:T(8,128)(2,1)S(1)}, u32[]{:S(2)}, u32[]{:S(2)}) collective-permute-start(bf16[512,768]{0,1:T(8,128)(2,1)S(1)} %slice.731), channel_id=1, source_target_pairs={{0,4},{4,0},{1,5},{5,1},{2,6},{6,2},{3,7},{7,3},{8,12},{12,8},{9,1... | collective-permute-start | bytes 2359304 | tf_op jit(solution)/shard_map/ppermute | solution.py:38
  556.7 56.6 %collective-permute-start.77 = (bf16[256,768]{0,1:T(8,128)(2,1)S(1)}, bf16[256,768]{0,1:T(8,128)(2,1)S(1)}, u32[]{:S(2)}, u32[]{:S(2)}) collective-permute-start(bf16[256,768]{0,1:T(8,128)(2,1)S(1)} %select_convert_fusion.1), channel_id=1, source_target_pairs={{0,2},{2,0},{1,3},{3,1},{4,6},{6,4},{5,7},{7,5},{8,10},{10,8},{9,1... | collective-permute-start | bytes 1179656 | tf_op jit(solution)/shard_map/ppermute | solution.py:38
  561.7 32.8 %collective-permute-start.49 = (bf16[128,2048]{1,0:T(8,128)(2,1)S(1)}, bf16[128,2048]{1,0:T(8,128)(2,1)S(1)}, u32[]{:S(2)}, u32[]{:S(2)}) collective-permute-start(bf16[128,2048]{1,0:T(8,128)(2,1)S(1)} %get-tuple-element.79), channel_id=1, source_target_pairs={{0,16},{16,0},{1,17},{17,1},{2,18},{18,2},{3,19},{19,3},{4,20},{20... | collective-permute-start | bytes 1572872 | tf_op jit(solution)/shard_map/ppermute | solution.py:38
  563.1 30.0 %collective-permute-start.50 = (bf16[128,2048]{1,0:T(8,128)(2,1)S(1)}, bf16[128,2048]{1,0:T(8,128)(2,1)S(1)}, u32[]{:S(2)}, u32[]{:S(2)}) collective-permute-start(bf16[128,2048]{1,0:T(8,128)(2,1)S(1)} %get-tuple-element.79), channel_id=1, source_target_pairs={{0,2},{2,0},{1,3},{3,1},{4,6},{6,4},{5,7},{7,5},{8,10},{10,8},{9,1... | collective-permute-start | bytes 1572872 | tf_op jit(solution)/shard_map/ppermute | solution.py:38
  591.3 22.2 %collective-permute-start.74 = (bf16[256,768]{0,1:T(8,128)(2,1)S(1)}, bf16[256,768]{0,1:T(8,128)(2,1)S(1)}, u32[]{:S(2)}, u32[]{:S(2)}) collective-permute-start(bf16[256,768]{0,1:T(8,128)(2,1)S(1)} %select_convert_fusion.2), channel_id=1, source_target_pairs={{0,2},{2,0},{1,3},{3,1},{4,6},{6,4},{5,7},{7,5},{8,10},{10,8},{9,1... | collective-permute-start | bytes 1179656 | tf_op jit(solution)/shard_map/ppermute | solution.py:38
  646.2 28.7 %collective-permute-start.54 = (bf16[2048,256]{1,0:T(8,128)(2,1)S(1)}, bf16[2048,256]{1,0:T(8,128)(2,1)S(1)}, u32[]{:S(2)}, u32[]{:S(2)}) collective-permute-start(bf16[2048,256]{1,0:T(8,128)(2,1)S(1)} %slice.384), channel_id=1, source_target_pairs={{0,1},{1,0},{2,3},{3,2},{4,5},{5,4},{6,7},{7,6},{8,9},{9,8},{10,11... | collective-permute-start | bytes 3145736 | tf_op jit(solution)/shard_map/ppermute | solution.py:38
  652.6 32.1 %collective-permute-start.69 = (bf16[256,1024]{1,0:T(8,128)(2,1)}, bf16[256,1024]{1,0:T(8,128)(2,1)}, u32[]{:S(2)}, u32[]{:S(2)}) collective-permute-start(bf16[256,1024]{1,0:T(8,128)(2,1)} %fusion.50), channel_id=1, source_target_pairs={{0,1},{1,0},{2,3},{3,2},{4,5},{5,4},{6,7},{7,6},{8,9},{9,8},{10,11... | collective-permute-start | bytes 1572872 | tf_op jit(solution)/shard_map/ppermute | solution.py:38
  676.1 29.5 %collective-permute-start.55 = (bf16[1024,256]{1,0:T(8,128)(2,1)}, bf16[1024,256]{1,0:T(8,128)(2,1)}, u32[]{:S(2)}, u32[]{:S(2)}) collective-permute-start(bf16[1024,256]{1,0:T(8,128)(2,1)} %slice.733), channel_id=1, source_target_pairs={{0,4},{4,0},{1,5},{5,1},{2,6},{6,2},{3,7},{7,3},{8,12},{12,8},{9,1... | collective-permute-start | bytes 1572872 | tf_op jit(solution)/shard_map/ppermute | solution.py:38
  688.0 32.8 %collective-permute-start.70 = (bf16[256,512]{1,0:T(8,128)(2,1)}, bf16[256,512]{1,0:T(8,128)(2,1)S(1)}, u32[]{:S(2)}, u32[]{:S(2)}) collective-permute-start(bf16[256,512]{1,0:T(8,128)(2,1)} %slice.734), channel_id=1, source_target_pairs={{0,4},{4,0},{1,5},{5,1},{2,6},{6,2},{3,7},{7,3},{8,12},{12,8},{9,1... | collective-permute-start | bytes 786440 | tf_op jit(solution)/shard_map/ppermute | solution.py:38
  711.8 24.2 %collective-permute-start.66 = (bf16[1024,512]{0,1:T(8,128)(2,1)}, bf16[1024,512]{0,1:T(8,128)(2,1)S(1)}, u32[]{:S(2)}, u32[]{:S(2)}) collective-permute-start(bf16[1024,512]{0,1:T(8,128)(2,1)} %fusion.44), channel_id=1, source_target_pairs={{0,1},{1,0},{2,3},{3,2},{4,5},{5,4},{6,7},{7,6},{8,9},{9,8},{10,11... | collective-permute-start | bytes 3145736 | tf_op jit(solution)/shard_map/ppermute | solution.py:38
  717.7 46.4 %collective-permute-start.56 = (bf16[512,2048]{1,0:T(8,128)(2,1)}, bf16[512,2048]{1,0:T(8,128)(2,1)S(1)}, u32[]{:S(2)}, u32[]{:S(2)}) collective-permute-start(bf16[512,2048]{1,0:T(8,128)(2,1)} %get-tuple-element.112), channel_id=1, source_target_pairs={{0,8},{8,0},{1,9},{9,1},{2,10},{10,2},{3,11},{11,3},{4,12},{12,4},... | collective-permute-start | bytes 6291464 | tf_op jit(solution)/shard_map/ppermute | solution.py:38
  739.2 24.7 %collective-permute-start.67 = (bf16[512,512]{0,1:T(8,128)(2,1)S(1)}, bf16[512,512]{0,1:T(8,128)(2,1)S(1)}, u32[]{:S(2)}, u32[]{:S(2)}) collective-permute-start(bf16[512,512]{0,1:T(8,128)(2,1)S(1)} %slice.732), channel_id=1, source_target_pairs={{0,4},{4,0},{1,5},{5,1},{2,6},{6,2},{3,7},{7,3},{8,12},{12,8},{9,1... | collective-permute-start | bytes 1572872 | tf_op jit(solution)/shard_map/ppermute | solution.py:38
  739.4 23.3 %collective-permute-start.65 = (f32[1,4352]{1,0:T(1,128)S(1)}, f32[1,4352]{1,0:T(1,128)S(1)}, u32[]{:S(2)}, u32[]{:S(2)}) collective-permute-start(f32[1,4352]{1,0:T(1,128)S(1)} %add.895), channel_id=1, source_target_pairs={{0,4},{4,0},{1,5},{5,1},{2,6},{6,2},{3,7},{7,3},{8,12},{12,8},{9,1... | collective-permute-start | bytes 52232 | tf_op jit(solution)/shard_map/ppermute | solution.py:38
  (104 other events, 1448.1 us)
